TPU v7x, 512 devices: a whole 4x4x16 slice. The times are simulated.
512 devices in a mesh: tile: 64 (over z_hi, x, y), plane: 8 (over z_lo, core).
Axes of the slice: x: 4, y: 4, z: 16 (z_hi: 4, z_lo: 4; z = z_hi * 4 + z_lo), core: 2. Of those that a mesh axis runs over, the one named last changes fastest.
Arguments:
- ref_feat: bfloat16 [32, 4, 16384], P(None, None, 'tile'), may hold values from -6 to 6
- src_feat: bfloat16 [4, 32, 4, 16384], P(None, 'plane', None, 'tile'), may hold values from -6 to 6
- shifts: int32 [4, 64], P(None, 'plane'), may hold values from 0 to 128, as said below
- conv_one: bfloat16 [8, 8, 3, 3, 3], replicated, may hold values from -0.4375 to 0.4375
- bias_one: float32 [8], replicated, may hold values from -0.5 to 0.5
- conv_two: bfloat16 [8, 8, 3, 3, 3], replicated, may hold values from -0.4375 to 0.4375
- bias_two: float32 [8], replicated, may hold values from -0.5 to 0.5
- view_head: float32 [8], replicated, may hold values from -2 to 2
Outputs:
- joined: bfloat16 [8, 64, 4, 16384], P(None, 'plane', None, 'tile')
Inputs may be any that keep to these rules, and one draw needn't show every extreme that they name: `shifts`: for every view the shift never falls from one plane to the next; it is 0 at plane 0 and 128 at plane 64 - 1.
All inputs are finite; a program needn't handle non-finite values.
Results may differ from a plain program's by a relative error of at most 0.0053.
Values may be sent and summed in bfloat16 or wider, within the bound.
A program may use at most 64 MiB of HBM per device.

v0:
```python
import jax
import jax.numpy as jnp
from jax import lax
from jax.sharding import PartitionSpec as P

CHANNELS = 32
GROUPS = 8
VIEWS = 4
MAX_SHIFT = 128


def padded(cells, sides, width):
    for axis, dim in sides:
        count = lax.axis_size(axis)
        ends = count - 1
        head = lax.slice_in_dim(cells, 0, width, axis=dim)
        tail = lax.slice_in_dim(cells, cells.shape[dim] - width, cells.shape[dim], axis=dim)
        cells = jnp.concatenate(
            [
                lax.ppermute(tail, axis, [(i, (i + 1) % count) for i in range(ends)]),
                cells,
                lax.ppermute(head, axis, [((i + 1) % count, i) for i in range(ends)]),
            ],
            axis=dim,
        )
    return cells


def from_behind(value, axis, by):
    peers = lax.axis_size(axis)
    pairs = [(i, i + by) for i in range(peers) if 0 <= i + by < peers]
    return lax.ppermute(value, axis, pairs)


def convolve_valid(volume, kernel):
    return lax.conv_general_dilated(
        volume[None],
        kernel,
        (1, 1, 1),
        "VALID",
        dimension_numbers=("NCDHW", "OIDHW", "NCDHW"),
        preferred_element_type=jnp.float32,
    )[0]


def margin_single(volume):
    return padded(volume, (("tile", 3), ("plane", 1)), 1)


def pad_rows(volume, depth):
    return jnp.pad(volume, ((0, 0), (0, 0), (depth, depth), (0, 0)))


def per_device(ref_feat, src_feat, shifts, conv_one, bias_one, conv_two, bias_two, view_head):
    tile_cols = ref_feat.shape[2]
    row_count = ref_feat.shape[1]
    planes = shifts.shape[1]
    gathered_all = lax.all_gather(src_feat, "plane", axis=1, tiled=True)
    before = from_behind(gathered_all[:, :, :, tile_cols - MAX_SHIFT :], "tile", 1)
    gathered = jnp.concatenate([before, gathered_all], axis=3)
    ref_wide = ref_feat.astype(jnp.float32)
    weighted = jnp.zeros((GROUPS, planes, row_count, tile_cols), jnp.float32)
    total_weight = jnp.zeros((planes, row_count, tile_cols), jnp.float32)
    for view_idx in range(VIEWS):
        source = gathered[view_idx]

        def one_plane(offset):
            start = MAX_SHIFT - offset
            shifted = lax.dynamic_slice_in_dim(source, start, tile_cols, 2).astype(jnp.float32)
            products = (ref_wide * shifted).reshape(
                GROUPS, CHANNELS // GROUPS, row_count, tile_cols
            )
            return jnp.mean(products, axis=1)

        matches = jnp.transpose(lax.map(one_plane, shifts[view_idx]), (1, 0, 2, 3)).astype(
            jnp.bfloat16
        )
        first_raw = convolve_valid(pad_rows(margin_single(matches), 1), conv_one)
        first_core = jax.nn.relu(first_raw + bias_one[:, None, None, None]).astype(jnp.bfloat16)
        first_out = pad_rows(margin_single(first_core), 1)
        second_out = jax.nn.relu(
            convolve_valid(first_out, conv_two) + bias_two[:, None, None, None]
        )
        scores = jnp.einsum("c,cdhw->dhw", view_head, second_out)
        weight = jax.nn.sigmoid(scores)
        weighted = weighted + weight[None] * matches.astype(jnp.float32)
        total_weight = total_weight + weight
    return (weighted / total_weight[None]).astype(jnp.bfloat16)


def solution(mesh):
    placed = (
        P(None, None, "tile"),
        P(None, "plane", None, "tile"),
        P(None, "plane"),
        P(),
        P(),
        P(),
        P(),
        P(),
    )
    return jax.shard_map(
        per_device,
        mesh=mesh,
        in_specs=placed,
        out_specs=P(None, "plane", None, "tile"),
        check_vma=False,
    )
```

profile of v0, /device:TPU:480, one launch (start us, length us, event | category | flops | bytes accessed | tf_op | source)
XLA Modules:
  0.0 421.3 jit_solution(3097313834694599378)
XLA Ops:
  0.0 14.6 %all_gather.3 = bf16[4,32,4,256]{3,2,1,0:T(4,128)(2,1)S(1)} all-gather(bf16[4,4,4,256]{3,2,1,0:T(4,128)(2,1)} %param.17), channel_id=1, replica_groups=mesh['tile'=64,'plane'=8] {'plane'}, dimensions={1}, use_global_device_ids=true | all-gather | bytes 294912 | tf_op jit(solution)/shard_map/all_gather | solution.py:58
  19.8 18.5 %collective-permute-done = bf16[4,32,4,128]{3,2,1,0:T(4,128)(2,1)S(1)} collective-permute-done((bf16[4,32,4,128]{3,2,1,0:T(4,128)(2,1)S(1)}, bf16[4,32,4,128]{3,2,1,0:T(4,128)(2,1)S(1)}, u32[]{:S(2)}, u32[]{:S(2)}) %collective-permute-start) | collective-permute-done | bytes 131104 | tf_op jit(solution)/shard_map/ppermute | solution.py:32
  38.7 16.5 %while.48 = (s32[]{:T(128)}, bf16[8,8,4,256]{3,2,0,1:T(4,128)(2,1)S(1)}, s32[8]{0:T(128)S(1)}, bf16[32,4,384]{2,1,0:T(4,128)(2,1)S(1)}, f32[32,4,256]{2,1,0:T(4,...) while((s32[]{:T(128)}, bf16[8,8,4,256]{3,2,0,1:T(4,128)(2,1)S(1)}, s32[8]{0:T(128)S(1)}, ...), condition=%wide.region_2.3_spmd, body=%wide.region_0.2_spmd.sunk | while | flops 98310 | bytes 295071 | solution.py:75
  57.3 12.0 %collective-permute-start.2 = (bf16[8,8,4,1]{3,2,1,0:T(4,128)(2,1)S(1)}, bf16[8,8,4,1]{3,2,1,0:T(4,128)(2,1)S(1)}, u32[]{:S(2)}, u32[]{:S(2)}) collective-permute-start(bf16[8,8,4,1]{3,2,1,0:T(4,128)(2,1)S(1)} %get-tuple-element.404), channel_id=1, source_target_pairs={{8,0},{16,8},{24,16},{32,24},{40,32},{48,40},{56,48},{64,56},{72,6... | collective-permute-start | bytes 1544 | tf_op jit(solution)/shard_map/ppermute | solution.py:22
  69.4 16.5 %while.50 = (s32[]{:T(128)}, bf16[8,8,4,256]{3,2,0,1:T(4,128)(2,1)S(1)}, s32[8]{0:T(128)S(1)}, bf16[32,4,384]{2,1,0:T(4,128)(2,1)S(1)}, f32[32,4,256]{2,1,0:T(4,...) while((s32[]{:T(128)}, bf16[8,8,4,256]{3,2,0,1:T(4,128)(2,1)S(1)}, s32[8]{0:T(128)S(1)}, ...), condition=%wide.region_8.9_spmd, body=%wide.region_6.8_spmd.sunk | while | flops 98310 | bytes 295071 | solution.py:75
  88.0 12.0 %collective-permute-start.18 = (bf16[8,8,4,1]{3,2,1,0:T(4,128)(2,1)S(1)}, bf16[8,8,4,1]{3,2,1,0:T(4,128)(2,1)S(1)}, u32[]{:S(2)}, u32[]{:S(2)}) collective-permute-start(bf16[8,8,4,1]{3,2,1,0:T(4,128)(2,1)S(1)} %get-tuple-element.396), channel_id=1, source_target_pairs={{8,0},{16,8},{24,16},{32,24},{40,32},{48,40},{56,48},{64,56},{72,6... | collective-permute-start | bytes 1544 | tf_op jit(solution)/shard_map/ppermute | solution.py:22
  100.1 15.0 %while.49 = (s32[]{:T(128)}, bf16[8,8,4,256]{3,2,0,1:T(4,128)(2,1)S(1)}, s32[8]{0:T(128)S(1)}, bf16[32,4,384]{2,1,0:T(4,128)(2,1)S(1)}, f32[32,4,256]{2,1,0:T(4,...) while((s32[]{:T(128)}, bf16[8,8,4,256]{3,2,0,1:T(4,128)(2,1)S(1)}, s32[8]{0:T(128)S(1)}, ...), condition=%wide.region_5.6_spmd, body=%wide.region_3.5_spmd.sunk | while | flops 98310 | bytes 295071 | solution.py:75
  117.1 16.7 %while.51 = (s32[]{:T(128)}, bf16[8,8,4,256]{3,2,0,1:T(4,128)(2,1)S(1)}, s32[8]{0:T(128)S(1)}, bf16[32,4,384]{2,1,0:T(4,128)(2,1)S(1)}, f32[32,4,256]{2,1,0:T(4,...) while((s32[]{:T(128)}, bf16[8,8,4,256]{3,2,0,1:T(4,128)(2,1)S(1)}, s32[8]{0:T(128)S(1)}, ...), condition=%wide.region_11.12_spmd, body=%wide.region_9.11_spmd.sunk | while | flops 98310 | bytes 295071 | solution.py:75
  139.9 12.0 %collective-permute-start.26 = (bf16[8,8,4,1]{3,2,1,0:T(4,128)(2,1)S(1)}, bf16[8,8,4,1]{3,2,1,0:T(4,128)(2,1)S(1)}, u32[]{:S(2)}, u32[]{:S(2)}) collective-permute-start(bf16[8,8,4,1]{3,2,1,0:T(4,128)(2,1)S(1)} %get-tuple-element.392), channel_id=1, source_target_pairs={{8,0},{16,8},{24,16},{32,24},{40,32},{48,40},{56,48},{64,56},{72,6... | collective-permute-start | bytes 1544 | tf_op jit(solution)/shard_map/ppermute | solution.py:22
  189.3 9.9 %broadcast_select_fusion.7 = f32[8,4,8,33,8]{4,2,3,1,0:T(8,128)} fusion(pred[8,33]{0,1:T(8,128)(4,1)S(1)} %copy-done.11, bf16[8,8,3,3,3]{1,0,4,3,2:T(8,128)(2,1)S(1)} %copy-done, bf16[8,10,6,1,7,2]{0,4,5,2,1,3:T(8,128)(2,1)S(1)} %slice.184, bf16[8,10,6,1,8,33]{0,4,5,2,1,3:T(8,128)(2,1)} %copy.97), kind=kOutput, calls=%fused_computation.76 | convolution fusion | flops 30070272 | bytes 540936 | tf_op jit(solution)/shard_map/conv_general_dilated | solution.py:36
  199.2 7.4 %broadcast_select_fusion.3 = f32[8,4,8,33,8]{4,2,3,1,0:T(8,128)} fusion(pred[8,33]{0,1:T(8,128)(4,1)S(1)} %copy-done.11, bf16[8,8,3,3,3]{1,0,4,3,2:T(8,128)(2,1)S(1)} %copy-done, bf16[8,10,6,1,7,2]{0,4,5,2,1,3:T(8,128)(2,1)S(1)} %slice.202, bf16[8,10,6,1,8,33]{0,4,5,2,1,3:T(8,128)(2,1)S(1)} %copy-done.2), kind=kOutput, calls=%fused_computation.72 | convolution fusion | flops 30070272 | bytes 540936 | tf_op jit(solution)/shard_map/conv_general_dilated | solution.py:36
  213.7 10.1 %broadcast_select_fusion.5 = f32[8,4,8,33,8]{4,2,3,1,0:T(8,128)} fusion(pred[8,33]{0,1:T(8,128)(4,1)S(1)} %copy-done.11, bf16[8,8,3,3,3]{1,0,4,3,2:T(8,128)(2,1)S(1)} %copy-done, bf16[8,10,6,1,7,2]{0,4,5,2,1,3:T(8,128)(2,1)S(1)} %slice.193, bf16[8,10,6,1,8,33]{0,4,5,2,1,3:T(8,128)(2,1)} %copy.106), kind=kOutput, calls=%fused_computation.74 | convolution fusion | flops 30070272 | bytes 540936 | tf_op jit(solution)/shard_map/conv_general_dilated | solution.py:36
  242.4 9.8 %broadcast_select_fusion.1 = f32[8,4,8,33,8]{4,2,3,1,0:T(8,128)} fusion(pred[8,33]{0,1:T(8,128)(4,1)S(1)} %copy-done.11, bf16[8,8,3,3,3]{1,0,4,3,2:T(8,128)(2,1)S(1)} %copy-done, bf16[8,10,6,1,7,2]{0,4,5,2,1,3:T(8,128)(2,1)S(1)} %slice.211, bf16[8,10,6,1,8,33]{0,4,5,2,1,3:T(8,128)(2,1)} %copy.124), kind=kOutput, calls=%fused_computation.70 | convolution fusion | flops 30070272 | bytes 540936 | tf_op jit(solution)/shard_map/conv_general_dilated | solution.py:36
  260.3 12.0 %collective-permute-start.14 = (bf16[8,8,4,1]{3,0,2,1:T(8,128)(2,1)S(1)}, bf16[8,8,4,1]{3,0,2,1:T(8,128)(2,1)S(1)}, u32[]{:S(2)}, u32[]{:S(2)}) collective-permute-start(bf16[8,8,4,1]{3,0,2,1:T(8,128)(2,1)S(1)} %get-tuple-element.398), channel_id=1, source_target_pairs={{8,0},{16,8},{24,16},{32,24},{40,32},{48,40},{56,48},{64,56},{72,6... | collective-permute-start | bytes 1544 | tf_op jit(solution)/shard_map/ppermute | solution.py:22
  274.4 12.0 %collective-permute-start.22 = (bf16[8,8,4,1]{3,0,2,1:T(8,128)(2,1)S(1)}, bf16[8,8,4,1]{3,0,2,1:T(8,128)(2,1)S(1)}, u32[]{:S(2)}, u32[]{:S(2)}) collective-permute-start(bf16[8,8,4,1]{3,0,2,1:T(8,128)(2,1)S(1)} %get-tuple-element.394), channel_id=1, source_target_pairs={{8,0},{16,8},{24,16},{32,24},{40,32},{48,40},{56,48},{64,56},{72,6... | collective-permute-start | bytes 1544 | tf_op jit(solution)/shard_map/ppermute | solution.py:22
  288.6 12.0 %collective-permute-start.30 = (bf16[8,8,4,1]{3,0,2,1:T(8,128)(2,1)S(1)}, bf16[8,8,4,1]{3,0,2,1:T(8,128)(2,1)S(1)}, u32[]{:S(2)}, u32[]{:S(2)}) collective-permute-start(bf16[8,8,4,1]{3,0,2,1:T(8,128)(2,1)S(1)} %get-tuple-element.390), channel_id=1, source_target_pairs={{8,0},{16,8},{24,16},{32,24},{40,32},{48,40},{56,48},{64,56},{72,6... | collective-permute-start | bytes 1544 | tf_op jit(solution)/shard_map/ppermute | solution.py:22
  302.7 12.0 %collective-permute-start.6 = (bf16[8,8,4,1]{3,0,2,1:T(8,128)(2,1)S(1)}, bf16[8,8,4,1]{3,0,2,1:T(8,128)(2,1)S(1)}, u32[]{:S(2)}, u32[]{:S(2)}) collective-permute-start(bf16[8,8,4,1]{3,0,2,1:T(8,128)(2,1)S(1)} %get-tuple-element.402), channel_id=1, source_target_pairs={{8,0},{16,8},{24,16},{32,24},{40,32},{48,40},{56,48},{64,56},{72,6... | collective-permute-start | bytes 1544 | tf_op jit(solution)/shard_map/ppermute | solution.py:22
  334.9 4.7 %copy.109 = bf16[8,10,6,1,8,33]{0,4,5,2,1,3:T(8,128)(2,1)} copy(bf16[8,10,6,1,8,33]{5,4,0,2,1,3:T(8,128)(2,1)S(1)} %reshape.118) | data formatting | bytes 506880 | tf_op jit(solution)/shard_map/conv_general_dilated | solution.py:36
  340.6 9.8 %broadcast_select_fusion.4 = f32[8,4,8,33,8]{4,2,3,1,0:T(8,128)} fusion(pred[8,33]{0,1:T(8,128)(4,1)S(1)} %copy-done.11, bf16[8,8,3,3,3]{1,0,4,3,2:T(8,128)(2,1)S(1)} %copy-done.10, bf16[8,10,6,1,7,2]{0,4,5,2,1,3:T(8,128)(2,1)S(1)} %slice.197, bf16[8,10,6,1,8,33]{0,4,5,2,1,3:T(8,128)(2,1)} %copy.109), kind=kOutput, calls=%fused_computation.73 | convolution fusion | flops 30070272 | bytes 540936 | tf_op jit(solution)/shard_map/conv_general_dilated | solution.py:36
  358.8 4.8 %copy.118 = bf16[8,10,6,1,8,33]{0,4,5,2,1,3:T(8,128)(2,1)} copy(bf16[8,10,6,1,8,33]{5,4,0,2,1,3:T(8,128)(2,1)S(1)} %reshape.132) | data formatting | bytes 506880 | tf_op jit(solution)/shard_map/conv_general_dilated | solution.py:36
  364.7 9.8 %broadcast_select_fusion.2 = f32[8,4,8,33,8]{4,2,3,1,0:T(8,128)} fusion(pred[8,33]{0,1:T(8,128)(4,1)S(1)} %copy-done.11, bf16[8,8,3,3,3]{1,0,4,3,2:T(8,128)(2,1)S(1)} %copy-done.10, bf16[8,10,6,1,7,2]{0,4,5,2,1,3:T(8,128)(2,1)S(1)} %slice.206, bf16[8,10,6,1,8,33]{0,4,5,2,1,3:T(8,128)(2,1)} %copy.118), kind=kOutput, calls=%fused_computation.71 | convolution fusion | flops 30070272 | bytes 540936 | tf_op jit(solution)/shard_map/conv_general_dilated | solution.py:36
  379.8 4.7 %copy.127 = bf16[8,10,6,1,8,33]{0,4,5,2,1,3:T(8,128)(2,1)} copy(bf16[8,10,6,1,8,33]{5,4,0,2,1,3:T(8,128)(2,1)S(1)} %reshape.146) | data formatting | bytes 506880 | tf_op jit(solution)/shard_map/conv_general_dilated | solution.py:36
  385.5 9.8 %broadcast_select_fusion = f32[8,4,8,33,8]{4,2,3,1,0:T(8,128)} fusion(pred[8,33]{0,1:T(8,128)(4,1)S(1)} %copy-done.11, bf16[8,8,3,3,3]{1,0,4,3,2:T(8,128)(2,1)S(1)} %copy-done.10, bf16[8,10,6,1,7,2]{0,4,5,2,1,3:T(8,128)(2,1)S(1)} %slice.215, bf16[8,10,6,1,8,33]{0,4,5,2,1,3:T(8,128)(2,1)} %copy.127), kind=kOutput, calls=%fused_computation.69 | convolution fusion | flops 30070272 | bytes 540936 | tf_op jit(solution)/shard_map/conv_general_dilated | solution.py:36
  406.0 10.0 %broadcast_select_fusion.6 = f32[8,4,8,33,8]{4,2,3,1,0:T(8,128)} fusion(pred[8,33]{0,1:T(8,128)(4,1)S(1)} %copy-done.11, bf16[8,8,3,3,3]{1,0,4,3,2:T(8,128)(2,1)S(1)} %copy-done.10, bf16[8,10,6,1,7,2]{0,4,5,2,1,3:T(8,128)(2,1)S(1)} %slice.188, bf16[8,10,6,1,8,33]{0,4,5,2,1,3:T(8,128)(2,1)} %copy.100), kind=kOutput, calls=%fused_computation.75 | convolution fusion | flops 30070272 | bytes 540936 | tf_op jit(solution)/shard_map/conv_general_dilated | solution.py:36
  (264 shorter events, 171.2 us)
Async XLA Ops:
  14.6 23.7 %collective-permute-start = (bf16[4,32,4,128]{3,2,1,0:T(4,128)(2,1)S(1)}, bf16[4,32,4,128]{3,2,1,0:T(4,128)(2,1)S(1)}, u32[]{:S(2)}, u32[]{:S(2)}) collective-permute-start(bf16[4,32,4,128]{3,2,1,0:T(4,128)(2,1)S(1)} %slice.180), channel_id=1, source_target_pairs={{0,8},{8,16},{16,24},{24,32},{32,40},{40,48},{48,56},{56,64},{64,7... | collective-permute-start | bytes 393224 | tf_op jit(solution)/shard_map/ppermute | solution.py:32
  55.4 78.6 %collective-permute-start.1 = (bf16[8,8,4,1]{3,2,1,0:T(4,128)(2,1)S(1)}, bf16[8,8,4,1]{3,2,1,0:T(4,128)(2,1)S(1)}, u32[]{:S(2)}, u32[]{:S(2)}) collective-permute-start(bf16[8,8,4,1]{3,2,1,0:T(4,128)(2,1)S(1)} %get-tuple-element.403), channel_id=1, source_target_pairs={{0,8},{8,16},{16,24},{24,32},{32,40},{40,48},{48,56},{56,64},{64,7... | collective-permute-start | bytes 1544 | tf_op jit(solution)/shard_map/ppermute | solution.py:20
  57.3 80.6 %collective-permute-start.2 = (bf16[8,8,4,1]{3,2,1,0:T(4,128)(2,1)S(1)}, bf16[8,8,4,1]{3,2,1,0:T(4,128)(2,1)S(1)}, u32[]{:S(2)}, u32[]{:S(2)}) collective-permute-start(bf16[8,8,4,1]{3,2,1,0:T(4,128)(2,1)S(1)} %get-tuple-element.404), channel_id=1, source_target_pairs={{8,0},{16,8},{24,16},{32,24},{40,32},{48,40},{56,48},{64,56},{72,6... | collective-permute-start | bytes 1544 | tf_op jit(solution)/shard_map/ppermute | solution.py:22
  86.0 53.9 %collective-permute-start.17 = (bf16[8,8,4,1]{3,2,1,0:T(4,128)(2,1)S(1)}, bf16[8,8,4,1]{3,2,1,0:T(4,128)(2,1)S(1)}, u32[]{:S(2)}, u32[]{:S(2)}) collective-permute-start(bf16[8,8,4,1]{3,2,1,0:T(4,128)(2,1)S(1)} %get-tuple-element.395), channel_id=1, source_target_pairs={{0,8},{8,16},{16,24},{24,32},{32,40},{40,48},{48,56},{56,64},{64,7... | collective-permute-start | bytes 1544 | tf_op jit(solution)/shard_map/ppermute | solution.py:20
  88.0 64.0 %collective-permute-start.18 = (bf16[8,8,4,1]{3,2,1,0:T(4,128)(2,1)S(1)}, bf16[8,8,4,1]{3,2,1,0:T(4,128)(2,1)S(1)}, u32[]{:S(2)}, u32[]{:S(2)}) collective-permute-start(bf16[8,8,4,1]{3,2,1,0:T(4,128)(2,1)S(1)} %get-tuple-element.396), channel_id=1, source_target_pairs={{8,0},{16,8},{24,16},{32,24},{40,32},{48,40},{56,48},{64,56},{72,6... | collective-permute-start | bytes 1544 | tf_op jit(solution)/shard_map/ppermute | solution.py:22
  115.2 38.9 %collective-permute-start.10 = (bf16[8,8,4,1]{3,2,1,0:T(4,128)(2,1)S(1)}, bf16[8,8,4,1]{3,2,1,0:T(4,128)(2,1)S(1)}, u32[]{:S(2)}, u32[]{:S(2)}) collective-permute-start(bf16[8,8,4,1]{3,2,1,0:T(4,128)(2,1)S(1)} %get-tuple-element.400), channel_id=1, source_target_pairs={{8,0},{16,8},{24,16},{32,24},{40,32},{48,40},{56,48},{64,56},{72,6... | collective-permute-start | bytes 1544 | tf_op jit(solution)/shard_map/ppermute | solution.py:22
  133.9 23.8 %collective-permute-start.9 = (bf16[8,8,4,1]{3,2,1,0:T(4,128)(2,1)S(1)}, bf16[8,8,4,1]{3,2,1,0:T(4,128)(2,1)S(1)}, u32[]{:S(2)}, u32[]{:S(2)}) collective-permute-start(bf16[8,8,4,1]{3,2,1,0:T(4,128)(2,1)S(1)} %get-tuple-element.399), channel_id=1, source_target_pairs={{0,8},{8,16},{16,24},{24,32},{32,40},{40,48},{48,56},{56,64},{64,7... | collective-permute-start | bytes 1544 | tf_op jit(solution)/shard_map/ppermute | solution.py:20
  139.9 23.5 %collective-permute-start.26 = (bf16[8,8,4,1]{3,2,1,0:T(4,128)(2,1)S(1)}, bf16[8,8,4,1]{3,2,1,0:T(4,128)(2,1)S(1)}, u32[]{:S(2)}, u32[]{:S(2)}) collective-permute-start(bf16[8,8,4,1]{3,2,1,0:T(4,128)(2,1)S(1)} %get-tuple-element.392), channel_id=1, source_target_pairs={{8,0},{16,8},{24,16},{32,24},{40,32},{48,40},{56,48},{64,56},{72,6... | collective-permute-start | bytes 1544 | tf_op jit(solution)/shard_map/ppermute | solution.py:22
  163.4 43.2 %collective-permute-start.11 = (bf16[8,1,4,258]{3,2,1,0:T(4,128)(2,1)S(1)}, bf16[8,1,4,258]{3,2,1,0:T(4,128)(2,1)S(1)}, u32[]{:S(2)}, u32[]{:S(2)}) collective-permute-start(bf16[8,1,4,258]{3,2,1,0:T(4,128)(2,1)S(1)} %get-tuple-element.383), channel_id=1, source_target_pairs={{0,1},{1,2},{2,3},{3,4},{4,5},{5,6},{6,7},{8,9},{9,10},{10,11},{11... | collective-permute-start | bytes 49544 | tf_op jit(solution)/shard_map/ppermute | solution.py:20
  165.5 41.2 %collective-permute-start.12 = (bf16[8,1,4,258]{3,2,1,0:T(4,128)(2,1)S(1)}, bf16[8,1,4,258]{3,2,1,0:T(4,128)(2,1)S(1)}, u32[]{:S(2)}, u32[]{:S(2)}) collective-permute-start(bf16[8,1,4,258]{3,2,1,0:T(4,128)(2,1)S(1)} %get-tuple-element.384), channel_id=1, source_target_pairs={{1,0},{2,1},{3,2},{4,3},{5,4},{6,5},{7,6},{9,8},{10,9},{11,10},{12... | collective-permute-start | bytes 49544 | tf_op jit(solution)/shard_map/ppermute | solution.py:22
  169.1 66.1 %collective-permute-start.27 = (bf16[8,1,4,258]{3,2,1,0:T(4,128)(2,1)S(1)}, bf16[8,1,4,258]{3,2,1,0:T(4,128)(2,1)S(1)}, u32[]{:S(2)}, u32[]{:S(2)}) collective-permute-start(bf16[8,1,4,258]{3,2,1,0:T(4,128)(2,1)S(1)} %get-tuple-element.375), channel_id=1, source_target_pairs={{0,1},{1,2},{2,3},{3,4},{4,5},{5,6},{6,7},{8,9},{9,10},{10,11},{11... | collective-permute-start | bytes 49544 | tf_op jit(solution)/shard_map/ppermute | solution.py:20
  178.3 57.0 %collective-permute-start.28 = (bf16[8,1,4,258]{3,2,1,0:T(4,128)(2,1)S(1)}, bf16[8,1,4,258]{3,2,1,0:T(4,128)(2,1)S(1)}, u32[]{:S(2)}, u32[]{:S(2)}) collective-permute-start(bf16[8,1,4,258]{3,2,1,0:T(4,128)(2,1)S(1)} %get-tuple-element.376), channel_id=1, source_target_pairs={{1,0},{2,1},{3,2},{4,3},{5,4},{6,5},{7,6},{9,8},{10,9},{11,10},{12... | collective-permute-start | bytes 49544 | tf_op jit(solution)/shard_map/ppermute | solution.py:22
  258.4 30.2 %collective-permute-start.13 = (bf16[8,8,4,1]{3,0,2,1:T(8,128)(2,1)S(1)}, bf16[8,8,4,1]{3,0,2,1:T(8,128)(2,1)S(1)}, u32[]{:S(2)}, u32[]{:S(2)}) collective-permute-start(bf16[8,8,4,1]{3,0,2,1:T(8,128)(2,1)S(1)} %get-tuple-element.397), channel_id=1, source_target_pairs={{0,8},{8,16},{16,24},{24,32},{32,40},{40,48},{48,56},{56,64},{64,7... | collective-permute-start | bytes 1544 | tf_op jit(solution)/shard_map/ppermute | solution.py:20
  260.3 40.3 %collective-permute-start.14 = (bf16[8,8,4,1]{3,0,2,1:T(8,128)(2,1)S(1)}, bf16[8,8,4,1]{3,0,2,1:T(8,128)(2,1)S(1)}, u32[]{:S(2)}, u32[]{:S(2)}) collective-permute-start(bf16[8,8,4,1]{3,0,2,1:T(8,128)(2,1)S(1)} %get-tuple-element.398), channel_id=1, source_target_pairs={{8,0},{16,8},{24,16},{32,24},{40,32},{48,40},{56,48},{64,56},{72,6... | collective-permute-start | bytes 1544 | tf_op jit(solution)/shard_map/ppermute | solution.py:22
  272.4 30.2 %collective-permute-start.21 = (bf16[8,8,4,1]{3,0,2,1:T(8,128)(2,1)S(1)}, bf16[8,8,4,1]{3,0,2,1:T(8,128)(2,1)S(1)}, u32[]{:S(2)}, u32[]{:S(2)}) collective-permute-start(bf16[8,8,4,1]{3,0,2,1:T(8,128)(2,1)S(1)} %get-tuple-element.393), channel_id=1, source_target_pairs={{0,8},{8,16},{16,24},{24,32},{32,40},{40,48},{48,56},{56,64},{64,7... | collective-permute-start | bytes 1544 | tf_op jit(solution)/shard_map/ppermute | solution.py:20
  274.4 40.3 %collective-permute-start.22 = (bf16[8,8,4,1]{3,0,2,1:T(8,128)(2,1)S(1)}, bf16[8,8,4,1]{3,0,2,1:T(8,128)(2,1)S(1)}, u32[]{:S(2)}, u32[]{:S(2)}) collective-permute-start(bf16[8,8,4,1]{3,0,2,1:T(8,128)(2,1)S(1)} %get-tuple-element.394), channel_id=1, source_target_pairs={{8,0},{16,8},{24,16},{32,24},{40,32},{48,40},{56,48},{64,56},{72,6... | collective-permute-start | bytes 1544 | tf_op jit(solution)/shard_map/ppermute | solution.py:22
  286.5 30.2 %collective-permute-start.29 = (bf16[8,8,4,1]{3,0,2,1:T(8,128)(2,1)S(1)}, bf16[8,8,4,1]{3,0,2,1:T(8,128)(2,1)S(1)}, u32[]{:S(2)}, u32[]{:S(2)}) collective-permute-start(bf16[8,8,4,1]{3,0,2,1:T(8,128)(2,1)S(1)} %get-tuple-element.389), channel_id=1, source_target_pairs={{0,8},{8,16},{16,24},{24,32},{32,40},{40,48},{48,56},{56,64},{64,7... | collective-permute-start | bytes 1544 | tf_op jit(solution)/shard_map/ppermute | solution.py:20
  288.6 31.9 %collective-permute-start.30 = (bf16[8,8,4,1]{3,0,2,1:T(8,128)(2,1)S(1)}, bf16[8,8,4,1]{3,0,2,1:T(8,128)(2,1)S(1)}, u32[]{:S(2)}, u32[]{:S(2)}) collective-permute-start(bf16[8,8,4,1]{3,0,2,1:T(8,128)(2,1)S(1)} %get-tuple-element.390), channel_id=1, source_target_pairs={{8,0},{16,8},{24,16},{32,24},{40,32},{48,40},{56,48},{64,56},{72,6... | collective-permute-start | bytes 1544 | tf_op jit(solution)/shard_map/ppermute | solution.py:22
  320.4 33.7 %collective-permute-start.23 = (bf16[8,1,4,258]{3,0,2,1:T(8,128)(2,1)S(1)}, bf16[8,1,4,258]{3,0,2,1:T(8,128)(2,1)S(1)}, u32[]{:S(2)}, u32[]{:S(2)}) collective-permute-start(bf16[8,1,4,258]{3,0,2,1:T(8,128)(2,1)S(1)} %get-tuple-element.377), channel_id=1, source_target_pairs={{0,1},{1,2},{2,3},{3,4},{4,5},{5,6},{6,7},{8,9},{9,10},{10,11},{11... | collective-permute-start | bytes 49544 | tf_op jit(solution)/shard_map/ppermute | solution.py:20
  322.5 35.4 %collective-permute-start.24 = (bf16[8,1,4,258]{3,0,2,1:T(8,128)(2,1)S(1)}, bf16[8,1,4,258]{3,0,2,1:T(8,128)(2,1)S(1)}, u32[]{:S(2)}, u32[]{:S(2)}) collective-permute-start(bf16[8,1,4,258]{3,0,2,1:T(8,128)(2,1)S(1)} %get-tuple-element.378), channel_id=1, source_target_pairs={{1,0},{2,1},{3,2},{4,3},{5,4},{6,5},{7,6},{9,8},{10,9},{11,10},{12... | collective-permute-start | bytes 49544 | tf_op jit(solution)/shard_map/ppermute | solution.py:22
  326.1 52.6 %collective-permute-start.31 = (bf16[8,1,4,258]{3,0,2,1:T(8,128)(2,1)S(1)}, bf16[8,1,4,258]{3,0,2,1:T(8,128)(2,1)S(1)}, u32[]{:S(2)}, u32[]{:S(2)}) collective-permute-start(bf16[8,1,4,258]{3,0,2,1:T(8,128)(2,1)S(1)} %get-tuple-element.373), channel_id=1, source_target_pairs={{0,1},{1,2},{2,3},{3,4},{4,5},{5,6},{6,7},{8,9},{9,10},{10,11},{11... | collective-permute-start | bytes 49544 | tf_op jit(solution)/shard_map/ppermute | solution.py:20
  328.3 50.5 %collective-permute-start.32 = (bf16[8,1,4,258]{3,0,2,1:T(8,128)(2,1)S(1)}, bf16[8,1,4,258]{3,0,2,1:T(8,128)(2,1)S(1)}, u32[]{:S(2)}, u32[]{:S(2)}) collective-permute-start(bf16[8,1,4,258]{3,0,2,1:T(8,128)(2,1)S(1)} %get-tuple-element.374), channel_id=1, source_target_pairs={{1,0},{2,1},{3,2},{4,3},{5,4},{6,5},{7,6},{9,8},{10,9},{11,10},{12... | collective-permute-start | bytes 49544 | tf_op jit(solution)/shard_map/ppermute | solution.py:22
  332.0 67.3 %collective-permute-start.7 = (bf16[8,1,4,258]{3,0,2,1:T(8,128)(2,1)S(1)}, bf16[8,1,4,258]{3,0,2,1:T(8,128)(2,1)S(1)}, u32[]{:S(2)}, u32[]{:S(2)}) collective-permute-start(bf16[8,1,4,258]{3,0,2,1:T(8,128)(2,1)S(1)} %get-tuple-element.385), channel_id=1, source_target_pairs={{0,1},{1,2},{2,3},{3,4},{4,5},{5,6},{6,7},{8,9},{9,10},{10,11},{11... | collective-permute-start | bytes 49544 | tf_op jit(solution)/shard_map/ppermute | solution.py:20
  354.2 45.1 %collective-permute-start.8 = (bf16[8,1,4,258]{3,0,2,1:T(8,128)(2,1)S(1)}, bf16[8,1,4,258]{3,0,2,1:T(8,128)(2,1)S(1)}, u32[]{:S(2)}, u32[]{:S(2)}) collective-permute-start(bf16[8,1,4,258]{3,0,2,1:T(8,128)(2,1)S(1)} %get-tuple-element.386), channel_id=1, source_target_pairs={{1,0},{2,1},{3,2},{4,3},{5,4},{6,5},{7,6},{9,8},{10,9},{11,10},{12... | collective-permute-start | bytes 49544 | tf_op jit(solution)/shard_map/ppermute | solution.py:22
  (21 other events, 640.5 us)
where the time goes:
time: 428 us; the launch traced here: 421 us
  starting transfers between devices  152 us (36%)
  local copies, waits for them, and re-layouts  106 us (25%)
  matrix products  77.5 us (18%)
  loops' own time  40.7 us (10%)
  waiting for transfers between devices  18.6 us (4%)
  blocking collectives  14.6 us (3%)
  other arithmetic  10.8 us (3%)
    ppermute x16, starting transfers between devices, padded(): lax.ppermute(head, axis, [((i + 1) % count, i) for i in range(ends)])  116 us
    conv_general_dilated x40, local copies, waits for them, and re-layouts, convolve_valid(): lax.conv_general_dilated(volume[None], kernel, (1, 1, 1), 'VALID', dimens...  83.7 us
    conv_general_dilated x8, matrix products, convolve_valid(): lax.conv_general_dilated(volume[None], kernel, (1, 1, 1), 'VALID', dimens...  76.6 us
    another operation x4, loops' own time, per_device(): lax.map(one_plane, shifts[view_idx])  40.7 us
    ppermute x16, starting transfers between devices, padded(): lax.ppermute(tail, axis, [(i, (i + 1) % count) for i in range(ends)])  32.9 us
    dynamic_slice x32, local copies, waits for them, and re-layouts, per_device(): lax.map(one_plane, shifts[view_idx])  19.5 us
    ppermute x1, waiting for transfers between devices, from_behind(): return lax.ppermute(value, axis, pairs)  18.5 us
    all_gather x1, blocking collectives, per_device(): gathered_all = lax.all_gather(src_feat, 'plane', axis=1, tiled=True)  14.6 us
  transfers between devices with their start and end apart: 33, of which 1 were waited for; matrix products, arithmetic and copies ran while one was open for 34% of the time, Pallas kernels for 0%

commit v1 on v0

v1 whole, which is shorter than its diff:
```python
import functools
import numpy as np
import jax
import jax.numpy as jnp
from jax import lax
from jax.experimental import pallas as pl
from jax.experimental.pallas import tpu as pltpu

VIEWS = 4
F32 = jnp.float32
BF16 = jnp.bfloat16


def placing():
    table = np.zeros((4, 256, 384), np.float32)
    for ho in range(4):
        for a in range(3):
            for b in range(3):
                hi = ho + b - 1
                if not 0 <= hi < 4:
                    continue
                for e in range(3):
                    for i in range(8):
                        table[ho, (a * 9 + b * 3 + e) * 8 + i, a * 96 + e * 32 + i * 4 + hi] = 1
    return table.reshape(1024, 384)


def banded(w_ref, place_ref, out_ref, steps):
    flat = jnp.concatenate([w_ref[tap].astype(F32) for tap in range(27)], axis=1)
    flat = jnp.concatenate([flat, jnp.zeros((8, 40), F32)], axis=1).astype(BF16)
    row = lax.broadcasted_iota(jnp.int32, (32, 8), 0)
    col = lax.broadcasted_iota(jnp.int32, (32, 8), 1)
    spread = (row // 4 == col).astype(F32).astype(BF16)
    wide = jnp.dot(spread, flat, preferred_element_type=F32)
    which = lax.broadcasted_iota(jnp.int32, (32, 256), 0) % 4
    wide = jnp.concatenate(
        [jnp.where(which == ho, wide, 0.0) for ho in range(4)], axis=1
    ).astype(BF16)
    base = jnp.dot(wide, place_ref[...], preferred_element_type=F32)
    base = jnp.concatenate([base, jnp.zeros((32, 384), F32)], axis=1)
    for do in range(steps):
        out_ref[do * 32 : do * 32 + 32, :] = pltpu.roll(base, 96 * do, 1).astype(BF16) if do else base.astype(BF16)


def per_row(ref):
    low = lax.broadcasted_iota(jnp.int32, (8, 128), 0) < 4
    return [jnp.where(low, ref[2 * q], ref[2 * q + 1]) for q in range(4)]


def compute(
    plane_axis, tile_axis, sh, g_ref, l_ref, e_ref, r_ref, w1_ref, w2_ref, place_ref, b1_ref, b2_ref,
    head_ref, o_ref, src, rf, w1, w2, x, f, acc, tot,
):
    p = lax.axis_index(plane_axis)
    t = lax.axis_index(tile_axis)
    last_p = lax.axis_size(plane_axis) - 1
    last_t = lax.axis_size(tile_axis) - 1
    lane = lax.broadcasted_iota(jnp.int32, (8, 128), 1)
    lane32 = lax.broadcasted_iota(jnp.int32, (32, 128), 1)
    sub = lax.broadcasted_iota(jnp.int32, (8, 128), 0)
    low = sub < 4
    banded(w1_ref, place_ref, w1, 5)
    banded(w2_ref, place_ref, w2, 4)
    for k in range(3):
        rf[k] = r_ref[:, k * 128 : k * 128 + 128].astype(F32) * 0.25
    bias_one, bias_two, head = per_row(b1_ref), per_row(b2_ref), per_row(head_ref)
    edge_keep = jnp.where(
        jnp.logical_or(jnp.logical_and(lane == 0, t < last_t), jnp.logical_and(lane == 127, t > 0)), 1.0, 0.0
    )

    def neighbours(tiles, lanes):
        n = len(tiles)
        right = [pltpu.roll(a, 1, 1) for a in tiles]
        left = [pltpu.roll(a, 127, 1) for a in tiles]
        return (
            [jnp.where(lanes == 0, right[(k - 1) % n], right[k]) for k in range(n)],
            tiles,
            [jnp.where(lanes == 127, left[(k + 1) % n], left[k]) for k in range(n)],
        )

    def one_view(v, carry):
        own = pl.ds(pl.multiple_of(v * 16, 16), 16)
        src[0] = jnp.where(t > 0, l_ref[:, own, :].reshape(128, 128).astype(F32), 0.0)
        both = g_ref[:, own, :].reshape(128, 256).astype(F32)
        src[1] = both[:, :128]
        src[2] = both[:, 128:]
        src[3] = e_ref[:, v].reshape(128, 128).astype(F32)

        def one_plane(d, carry):
            s = sh[v, d]
            inside = jnp.logical_and(
                jnp.logical_or(d >= 2, p > 0), jnp.logical_or(d < 10, p < last_p)
            )
            scale = jnp.where(inside, 1.0, 0.0)
            before = lane32 < s
            parts = [[], [], []]
            for q in range(4):
                rows = slice(32 * q, 32 * q + 32)
                r = [pltpu.roll(src[k, rows, :], s, 1) for k in range(4)]
                tiles = (
                    jnp.where(before, r[0], r[1]),
                    jnp.where(before, r[1], r[2]),
                    jnp.where(
                        lane32 < 64, jnp.where(before, r[2], r[3]), jnp.where(before, r[3], r[0])
                    ),
                )
                for k in range(3):
                    prod = tiles[k] * rf[k, rows, :]
                    v0 = prod[0:8] + prod[8:16]
                    v1 = prod[16:24] + prod[24:32]
                    both = jnp.where(low, v0, v1) + pltpu.roll(jnp.where(low, v1, v0), 4, 0)
                    parts[k].append(both * scale)
            tiles = [jnp.concatenate(parts[k], axis=0) for k in range(3)]
            base = pl.multiple_of(d * 96, 32)
            for e, moved in enumerate(neighbours(tiles, lane32)):
                for k in range(3):
                    x[pl.ds(base + e * 32, 32), k * 128 : k * 128 + 128] = moved[k].astype(BF16)
            return carry

        lax.fori_loop(0, 12, one_plane, 0, unroll=2)

        for j in range(2):
            raw = jnp.dot(
                w1[:, :672], x[j * 480 : j * 480 + 672, :], preferred_element_type=F32
            )
            for i in range(5):
                d = j * 5 + i
                tiles = []
                for k in range(3):
                    cols = slice(k * 128, k * 128 + 128)
                    rows = []
                    for q in range(4):
                        at = i * 32 + q * 8
                        val = jnp.maximum(raw[at : at + 8, cols] + bias_one[q], 0.0)
                        if k == 2:
                            val = val * edge_keep
                        if d == 0:
                            val = jnp.where(p > 0, val, 0.0)
                        if d == 9:
                            val = jnp.where(p < last_p, val, 0.0)
                        rows.append(val)
                    tiles.append(jnp.concatenate(rows, axis=0))
                for e, moved in enumerate(neighbours(tiles, lane32)):
                    for k in range(2):
                        f[d * 96 + e * 32 : d * 96 + e * 32 + 32, k * 128 : k * 128 + 128] = moved[k].astype(BF16)

        for j in range(2):
            raw = jnp.dot(w2[:, :576], f[j * 384 : j * 384 + 576, :], preferred_element_type=F32)
            for i in range(4):
                d = j * 4 + i
                for k in range(2):
                    cols = slice(k * 128, k * 128 + 128)
                    score = None
                    for q in range(4):
                        at = i * 32 + q * 8
                        term = jnp.maximum(raw[at : at + 8, cols] + bias_two[q], 0.0) * head[q]
                        score = term if score is None else score + term
                    score = score + pltpu.roll(score, 4, 0)
                    weight = 1.0 / (1.0 + jnp.exp(-score))
                    at = (d + 2) * 96 + 32
                    match = x[at : at + 32, cols].astype(F32)
                    tot[d, :, cols] = tot[d, :, cols] + weight
                    for q in range(4):
                        rows = slice(q * 8, q * 8 + 8)
                        acc[d, rows, cols] = acc[d, rows, cols] + weight * match[rows]
        return carry

    acc[...] = jnp.zeros_like(acc)
    tot[...] = jnp.zeros_like(tot)
    lax.fori_loop(0, VIEWS, one_view, 0)
    for d in range(8):
        for q in range(4):
            val = (acc[d, q * 8 : q * 8 + 8, :] / tot[d]).astype(BF16)
            o_ref[2 * q, d] = val[0:4]
            o_ref[2 * q + 1, d] = val[4:8]


def call_compute(plane_axis, tile_axis, sh, g, l, e, r, w1, w2, b1, b2, head):
    smem = pl.BlockSpec(memory_space=pltpu.SMEM)
    vmem = pl.BlockSpec(memory_space=pltpu.VMEM)
    place = jnp.asarray(placing(), BF16)
    return pl.pallas_call(
        functools.partial(compute, plane_axis, tile_axis),
        out_shape=jax.ShapeDtypeStruct((8, 8, 4, 256), BF16),
        in_specs=[smem, vmem, vmem, vmem, vmem, vmem, vmem, vmem, smem, smem, smem],
        out_specs=vmem,
        scratch_shapes=[
            pltpu.VMEM((4, 128, 128), F32),
            pltpu.VMEM((3, 128, 128), F32),
            pltpu.VMEM((160, 768), BF16),
            pltpu.VMEM((128, 768), BF16),
            pltpu.VMEM((1152, 384), BF16),
            pltpu.VMEM((960, 256), BF16),
            pltpu.VMEM((8, 32, 256), F32),
            pltpu.VMEM((8, 8, 256), F32),
        ],
        compiler_params=pltpu.CompilerParams(vmem_limit_bytes=40 << 20),
        name="cost_volume",
    )(sh, g, l, e, r, w1, w2, place, b1, b2, head)


MESH = pl.DeviceIdType.MESH


def exchange(pack_ref, g_ref, l_ref, r_ref, send, recv, pass_send, pass_recv, own_sem):
    t, p = lax.axis_index("tile"), lax.axis_index("plane")
    last = lax.axis_size("tile") - 1
    chip, core = p // 2, p % 2
    other = chip * 2 + 1 - core
    peers = [other] + [(chip + dz) % 4 * 2 + core for dz in range(1, 4)]
    sources = [other] + [(chip + 4 - dz) % 4 * 2 + core for dz in range(1, 4)]

    barrier = pltpu.get_barrier_semaphore()

    def greet(tile, plane):
        pl.semaphore_signal(barrier, inc=1, device_id=(tile, plane), device_id_type=MESH)

    @pl.when(t < last)
    def _():
        greet(t + 1, p)

    @pl.when(t > 0)
    def _():
        greet(t - 1, p)

    for dz in range(4):
        greet(t, peers[dz])

    sides = jnp.where(t < last, 1, 0) + jnp.where(t > 0, 1, 0)
    pl.semaphore_wait(barrier, 4 + sides)

    def copy(src, dst, from_sem, to_sem, tile, plane):
        return pltpu.make_async_remote_copy(
            src_ref=src, dst_ref=dst, send_sem=from_sem, recv_sem=to_sem,
            device_id=(tile, plane), device_id_type=MESH,
        )

    right = copy(pack_ref.at[:, 128:256], l_ref.at[p], send.at[0, 4], recv.at[0, 4], t + 1, p)
    left = copy(pack_ref.at[64:72, 0:128], r_ref.at[p], send.at[1, 4], recv.at[1, 4], t - 1, p)
    bufs = (g_ref, l_ref, r_ref)

    def spread(kind, dz):
        src = pack_ref if kind == 0 else bufs[kind].at[p]
        return copy(src, bufs[kind].at[p], send.at[kind, dz], recv.at[kind, dz], t, peers[dz])

    def passing(kind, dz):
        slot = bufs[kind].at[sources[dz]]
        return copy(slot, slot, pass_send.at[kind, dz], pass_recv.at[kind, dz], t, other)

    mine = pltpu.make_async_copy(pack_ref, g_ref.at[p], own_sem)

    @pl.when(t < last)
    def _():
        right.start()

    @pl.when(t > 0)
    def _():
        left.start()

    for dz in (2, 1, 3, 0):
        spread(0, dz).start()
    mine.start()

    @pl.when(t > 0)
    def _():
        right.wait_recv()
        for dz in (2, 1, 3, 0):
            spread(1, dz).start()

    @pl.when(t < last)
    def _():
        left.wait_recv()
        for dz in (2, 1, 3, 0):
            spread(2, dz).start()

    def relay(kind):
        for dz in (1, 3, 2):
            spread(kind, dz).wait_recv()
            passing(kind, dz).start()

    def finish(kind):
        spread(kind, 0).wait_recv()
        for dz in range(4):
            spread(kind, dz).wait_send()
        for dz in (1, 3, 2):
            passing(kind, dz).wait()

    relay(0)

    @pl.when(t > 0)
    def _():
        relay(1)

    @pl.when(t < last)
    def _():
        relay(2)

    mine.wait()
    finish(0)

    @pl.when(t > 0)
    def _():
        finish(1)
        left.wait_send()

    @pl.when(t < last)
    def _():
        finish(2)
        right.wait_send()


def call_exchange(pack):
    vmem = pl.BlockSpec(memory_space=pltpu.VMEM)
    return pl.pallas_call(
        exchange,
        out_shape=[
            jax.ShapeDtypeStruct((8, 72, 256), BF16),
            jax.ShapeDtypeStruct((8, 72, 128), BF16),
            jax.ShapeDtypeStruct((8, 8, 128), BF16),
        ],
        in_specs=[vmem],
        out_specs=[vmem, vmem, vmem],
        scratch_shapes=[
            pltpu.SemaphoreType.DMA((3, 5)),
            pltpu.SemaphoreType.DMA((3, 5)),
            pltpu.SemaphoreType.DMA((3, 4)),
            pltpu.SemaphoreType.DMA((3, 4)),
            pltpu.SemaphoreType.DMA,
        ],
        compiler_params=pltpu.CompilerParams(
            collective_id=0, has_side_effects=True, vmem_limit_bytes=8 << 20
        ),
        name="exchange",
    )(pack)


def per_device(ref_feat, src_feat, shifts, conv_one, bias_one, conv_two, bias_two, view_head):
    t, p = lax.axis_index("tile"), lax.axis_index("plane")
    last_t = lax.axis_size("tile") - 1
    ref_rows = ref_feat.reshape(128, 256)
    src_rows = src_feat.reshape(64, 256)

    def side(at, more):
        lo = jnp.pad(src_rows[:, at : at + 2].T, ((0, 0), (0, 64)))
        at = at if at == 0 else 254
        hi = ref_rows[:, at : at + 2].T
        return jnp.concatenate([lo, hi, more], axis=0)

    whole = jnp.pad(shifts.reshape(1, 32).astype(BF16), ((0, 3), (0, 96)))
    extra = jnp.concatenate([side(0, whole), side(126, jnp.zeros((4, 128), BF16))], axis=1)
    pack = jnp.concatenate([src_rows, extra], axis=0)
    g, l, r = call_exchange(pack)

    def columns(rows):
        return jnp.transpose(rows.reshape(8, 2, 4, 16), (0, 2, 3, 1))

    el = columns(jnp.where(t > 0, l[:, 64:66, :64], 0))
    er = columns(jnp.where(t < last_t, r[:, 0:2, :64], 0))
    e = jnp.concatenate([er, jnp.zeros((8, 4, 16, 124), BF16), el], axis=-1)
    rl = jnp.where(t > 0, l[0, 66:68, :], 0).T
    rr = jnp.where(t < last_t, r[0, 2:4, :], 0).T
    ref_wide = jnp.concatenate([ref_rows, rr, jnp.zeros((128, 124), BF16), rl], axis=1)
    every = g[:, 68, :32].astype(jnp.int32).reshape(8, 4, 8)
    every = jnp.pad(jnp.transpose(every, (1, 0, 2)).reshape(4, 64), ((0, 0), (2, 2)))
    sh = lax.dynamic_slice_in_dim(every, p * 8, 12, 1)
    kernel_of = lambda w: jnp.transpose(w, (2, 3, 4, 0, 1)).reshape(27, 8, 8)
    return call_compute(
        "plane", "tile", sh, g, l, e, ref_wide,
        kernel_of(conv_one), kernel_of(conv_two), bias_one, bias_two, view_head,
    )


def solution(mesh):
    from jax.sharding import PartitionSpec as P
    placed = (
        P(None, None, "tile"), P(None, "plane", None, "tile"), P(None, "plane"),
        P(), P(), P(), P(), P(),
    )
    return jax.shard_map(
        per_device, mesh=mesh, in_specs=placed, out_specs=P(None, "plane", None, "tile"), check_vma=False,
    )
```

time: 428 us -> 40 us (0.09)
  the two profiles are of different devices: /device:TPU:480 before, /device:TPU:129 now
where the time goes in v1:
time: 40 us; the launch traced here: 39.7 us
  Pallas kernels  35.5 us (89%)
  local copies, waits for them, and re-layouts  3.77 us (9%)
    pallas_call x1, Pallas kernels, call_exchange(): pl.pallas_call(exchange, out_shape=[jax.ShapeDtypeStruct((8, 72, 256), BF...  21.4 us
    pallas_call x1, Pallas kernels, call_compute(): pl.pallas_call(functools.partial(compute, plane_axis, tile_axis), out_sha...  14.1 us
    unnamed x18, local copies, waits for them, and re-layouts  1.5 us

profile of v1, /device:TPU:129, one launch (start us, length us, event | category | flops | bytes accessed | tf_op | source)
XLA Modules:
  0.0 39.7 jit_solution(13148824463686339702)
XLA Ops:
  0.0 0.8 %reshape.46 = bf16[64,256]{1,0:T(8,128)(2,1)S(1)} reshape(bf16[4,4,4,256]{3,2,1,0:T(4,128)(2,1)} %param.10) | data formatting | bytes 65536 | tf_op jit(solution)/shard_map/reshape | solution.py:341
  0.8 0.1 fusion.16
  0.9 0.1 copy.29
  0.9 0.6 %copy-done.7 = s32[4,8]{1,0:T(4,128)S(1)} copy-done((s32[4,8]{1,0:T(4,128)S(1)}, s32[4,8]{1,0:T(4,128)}, u32[]{:S(2)}) %copy-start.7) | copy-done | bytes 152
  1.6 0.1 convert_element_type.31
  1.6 0.1 copy.28
  1.8 0.1 slice_bitcast_fusion.1
  1.9 0.1 copy.22
  1.9 0.1 copy.20
  2.1 21.4 %exchange.1 = (bf16[8,72,256]{2,1,0:T(8,128)(2,1)S(1)}, bf16[8,72,128]{2,1,0:T(8,128)(2,1)S(1)}, bf16[8,8,128]{2,1,0:T(8,128)(2,1)S(1)}) custom-call(bf16[72,256]{1,0:T(8,128)(2,1)S(1)} %fusion.11.pack_ref), custom_call_target="tpu_custom_call" | custom-call | tf_op jit(solution)/shard_map/exchange/pallas_call | solution.py:314
  23.5 0.1 convert_element_type.32
  23.6 0.1 reshape.48
  23.7 0.1 pad_convert_fusion
  23.7 0.1 constant_dynamic-slice_fusion.sh
  23.8 0.2 copy.25
  24.0 0.2 copy.24
  24.2 0.1 pad.28.clone
  24.3 0.1 pad_maximum_fusion.e_ref
  24.4 0.1 copy.27
  24.5 0.1 copy.26
  24.7 0.1 pad.25.clone
  24.8 0.1 pad_maximum_fusion.1.r_ref
  24.9 0.7 %copy-done.1 = bf16[8,8,3,3,3]{1,0,4,3,2:T(8,128)(2,1)S(1)} copy-done((bf16[8,8,3,3,3]{1,0,4,3,2:T(8,128)(2,1)S(1)}, bf16[8,8,3,3,3]{1,0,4,3,2:T(8,128)(2,1)}, u32[]{:S(2)}) %copy-start.1) | copy-done | bytes 3480
  25.6 14.1 %cost_volume.1 = bf16[8,8,4,256]{3,2,1,0:T(4,128)(2,1)} custom-call(s32[4,12]{1,0:T(4,128)S(1)} %constant_dynamic-slice_fusion.sh, bf16[8,72,256]{2,1,0:T(8,128)(2,1)S(1)} %get-tuple-element.8.g_ref, bf16[8,72,128]{2,1,0:T(8,128)(2,1)S(1)} %get-tuple-element.9.l_ref, bf16[8,4,16,128]{3,2,1,0:T(8,128)(2,1)S(1)} %pad_maximum_fusion.e_ref, ...), custom_call_target="tpu_custom_call" | custom-call | tf_op jit(solution)/shard_map/cost_volume/pallas_call | solution.py:182
  (25 shorter events, 0.2 us)
Async XLA Ops:
  0.8 1.0 %copy-start.6 = (bf16[32,4,256]{2,1,0:T(4,128)(2,1)S(1)}, bf16[32,4,256]{2,1,0:T(4,128)(2,1)}, u32[]{:S(2)}) copy-start(bf16[32,4,256]{2,1,0:T(4,128)(2,1)} %param.9) | copy-start | bytes 196612
  0.9 0.7 %copy-start.7 = (s32[4,8]{1,0:T(4,128)S(1)}, s32[4,8]{1,0:T(4,128)}, u32[]{:S(2)}) copy-start(s32[4,8]{1,0:T(4,128)} %param.11) | copy-start | bytes 388
  1.8 23.1 %copy-start = (bf16[1024,384]{1,0:T(8,128)(2,1)S(1)}, bf16[1024,384]{1,0:T(8,128)(2,1)}, u32[]{:S(2)}) copy-start(bf16[1024,384]{1,0:T(8,128)(2,1)} %constant.25.clone.place_ref) | copy-start | bytes 2359300
  24.8 0.8 %copy-start.1 = (bf16[8,8,3,3,3]{1,0,4,3,2:T(8,128)(2,1)S(1)}, bf16[8,8,3,3,3]{1,0,4,3,2:T(8,128)(2,1)}, u32[]{:S(2)}) copy-start(bf16[8,8,3,3,3]{1,0,4,3,2:T(8,128)(2,1)} %param.12) | copy-start | bytes 10372
  24.8 0.8 %copy-start.2 = (bf16[8,8,3,3,3]{1,0,4,3,2:T(8,128)(2,1)S(1)}, bf16[8,8,3,3,3]{1,0,4,3,2:T(8,128)(2,1)}, u32[]{:S(2)}) copy-start(bf16[8,8,3,3,3]{1,0,4,3,2:T(8,128)(2,1)} %param.14) | copy-start | bytes 10372
  24.9 0.8 %copy-start.3 = (f32[8]{0:T(128)S(1)}, f32[8]{0:T(128)}, u32[]{:S(2)}) copy-start(f32[8]{0:T(128)} %b1_ref.1) | copy-start | bytes 100
  24.9 0.7 %copy-start.4 = (f32[8]{0:T(128)S(1)}, f32[8]{0:T(128)}, u32[]{:S(2)}) copy-start(f32[8]{0:T(128)} %b2_ref.1) | copy-start | bytes 100
  24.9 0.7 %copy-start.5 = (f32[8]{0:T(128)S(1)}, f32[8]{0:T(128)}, u32[]{:S(2)}) copy-start(f32[8]{0:T(128)} %head_ref.1) | copy-start | bytes 100

commit v2 on v1

--- a/solution.py
+++ b/solution.py
@@ -49,7 +49,7 @@
 
 def compute(
     plane_axis, tile_axis, sh, g_ref, l_ref, e_ref, r_ref, w1_ref, w2_ref, place_ref, b1_ref, b2_ref,
-    head_ref, o_ref, src, rf, w1, w2, x, f, acc, tot,
+    head_ref, o_ref, src2, rf, w1, w2, x2, f2, acc, tot,
 ):
     p = lax.axis_index(plane_axis)
     t = lax.axis_index(tile_axis)
@@ -70,6 +70,7 @@
 
     def neighbours(tiles, lanes):
         n = len(tiles)
+        tiles = [a.astype(BF16) for a in tiles]
         right = [pltpu.roll(a, 1, 1) for a in tiles]
         left = [pltpu.roll(a, 127, 1) for a in tiles]
         return (
@@ -78,21 +79,19 @@
             [jnp.where(lanes == 127, left[(k + 1) % n], left[k]) for k in range(n)],
         )
 
-    def one_view(v, carry):
+    def one_view(v, xs, f):
+        x, src = xs, src2
         own = pl.ds(pl.multiple_of(v * 16, 16), 16)
-        src[0] = jnp.where(t > 0, l_ref[:, own, :].reshape(128, 128).astype(F32), 0.0)
-        both = g_ref[:, own, :].reshape(128, 256).astype(F32)
+        src[0] = jnp.where(t > 0, l_ref[:, own, :].reshape(128, 128), jnp.zeros((128, 128), BF16))
+        both = g_ref[:, own, :].reshape(128, 256)
         src[1] = both[:, :128]
         src[2] = both[:, 128:]
-        src[3] = e_ref[:, v].reshape(128, 128).astype(F32)
-
-        def one_plane(d, carry):
+        src[3] = e_ref[:, v].reshape(128, 128)
+
+        def one_plane(d):
             s = sh[v, d]
-            inside = jnp.logical_and(
-                jnp.logical_or(d >= 2, p > 0), jnp.logical_or(d < 10, p < last_p)
-            )
-            scale = jnp.where(inside, 1.0, 0.0)
             before = lane32 < s
+            outer = jnp.logical_xor(before, lane32 < 64)
             parts = [[], [], []]
             for q in range(4):
                 rows = slice(32 * q, 32 * q + 32)
@@ -100,24 +99,26 @@
                 tiles = (
                     jnp.where(before, r[0], r[1]),
                     jnp.where(before, r[1], r[2]),
-                    jnp.where(
-                        lane32 < 64, jnp.where(before, r[2], r[3]), jnp.where(before, r[3], r[0])
-                    ),
+                    jnp.where(outer, r[3], jnp.where(lane32 < 64, r[2], r[0])),
                 )
                 for k in range(3):
-                    prod = tiles[k] * rf[k, rows, :]
+                    prod = tiles[k].astype(F32) * rf[k, rows, :]
                     v0 = prod[0:8] + prod[8:16]
                     v1 = prod[16:24] + prod[24:32]
                     both = jnp.where(low, v0, v1) + pltpu.roll(jnp.where(low, v1, v0), 4, 0)
-                    parts[k].append(both * scale)
+                    parts[k].append(both)
             tiles = [jnp.concatenate(parts[k], axis=0) for k in range(3)]
-            base = pl.multiple_of(d * 96, 32)
+            if d < 2:
+                tiles = [jnp.where(p > 0, a, 0.0) for a in tiles]
+            if d > 9:
+                tiles = [jnp.where(p < last_p, a, 0.0) for a in tiles]
+            base = d * 96
             for e, moved in enumerate(neighbours(tiles, lane32)):
                 for k in range(3):
-                    x[pl.ds(base + e * 32, 32), k * 128 : k * 128 + 128] = moved[k].astype(BF16)
-            return carry
-
-        lax.fori_loop(0, 12, one_plane, 0, unroll=2)
+                    x[base + e * 32 : base + e * 32 + 32, k * 128 : k * 128 + 128] = moved[k]
+
+        for d in range(12):
+            one_plane(d)
 
         for j in range(2):
             raw = jnp.dot(
@@ -142,7 +143,7 @@
                     tiles.append(jnp.concatenate(rows, axis=0))
                 for e, moved in enumerate(neighbours(tiles, lane32)):
                     for k in range(2):
-                        f[d * 96 + e * 32 : d * 96 + e * 32 + 32, k * 128 : k * 128 + 128] = moved[k].astype(BF16)
+                        f[d * 96 + e * 32 : d * 96 + e * 32 + 32, k * 128 : k * 128 + 128] = moved[k]
 
         for j in range(2):
             raw = jnp.dot(w2[:, :576], f[j * 384 : j * 384 + 576, :], preferred_element_type=F32)
@@ -163,11 +164,16 @@
                     for q in range(4):
                         rows = slice(q * 8, q * 8 + 8)
                         acc[d, rows, cols] = acc[d, rows, cols] + weight * match[rows]
+
+    def two_views(i, carry):
+        for k in range(2):
+            one_view(i * 2 + k, x2.at[k], f2.at[k])
         return carry
 
     acc[...] = jnp.zeros_like(acc)
     tot[...] = jnp.zeros_like(tot)
-    lax.fori_loop(0, VIEWS, one_view, 0)
+    two_views(0, 0)
+    two_views(1, 0)
     for d in range(8):
         for q in range(4):
             val = (acc[d, q * 8 : q * 8 + 8, :] / tot[d]).astype(BF16)
@@ -185,12 +191,12 @@
         in_specs=[smem, vmem, vmem, vmem, vmem, vmem, vmem, vmem, smem, smem, smem],
         out_specs=vmem,
         scratch_shapes=[
-            pltpu.VMEM((4, 128, 128), F32),
+            pltpu.VMEM((4, 128, 128), BF16),
             pltpu.VMEM((3, 128, 128), F32),
             pltpu.VMEM((160, 768), BF16),
             pltpu.VMEM((128, 768), BF16),
-            pltpu.VMEM((1152, 384), BF16),
-            pltpu.VMEM((960, 256), BF16),
+            pltpu.VMEM((2, 1152, 384), BF16),
+            pltpu.VMEM((2, 960, 256), BF16),
             pltpu.VMEM((8, 32, 256), F32),
             pltpu.VMEM((8, 8, 256), F32),
         ],

time: 40 us -> 33.8 us (0.84)
  Pallas kernels: 35.5 us -> 29.3 us
    pallas_call x1, Pallas kernels: 14.1 us -> 7.9 us  [call_compute(): pl.pallas_call(functools.partial(compute, plane_axis, tile_axis), out_sha...]
where the time goes in v2:
time: 33.8 us; the launch traced here: 33.5 us
  Pallas kernels  29.3 us (87%)
  local copies, waits for them, and re-layouts  3.77 us (11%)
  other arithmetic  0.34 us (1%)
    pallas_call x1, Pallas kernels, call_exchange(): pl.pallas_call(exchange, out_shape=[jax.ShapeDtypeStruct((8, 72, 256), BF...  21.4 us
    pallas_call x1, Pallas kernels, call_compute(): pl.pallas_call(functools.partial(compute, plane_axis, tile_axis), out_sha...  7.9 us
    unnamed x18, local copies, waits for them, and re-layouts  1.5 us
    reshape x1, local copies, waits for them, and re-layouts, per_device(): src_rows = src_feat.reshape(64, 256)  0.77 us

profile of v2, /device:TPU:129, one launch (start us, length us, event | category | flops | bytes accessed | tf_op | source)
XLA Modules:
  0.0 33.5 jit_solution(16267914082014412090)
XLA Ops:
  0.0 0.8 %reshape.46 = bf16[64,256]{1,0:T(8,128)(2,1)S(1)} reshape(bf16[4,4,4,256]{3,2,1,0:T(4,128)(2,1)} %param.10) | data formatting | bytes 65536 | tf_op jit(solution)/shard_map/reshape | solution.py:347
  0.8 0.1 fusion.16
  0.9 0.1 copy.29
  0.9 0.6 %copy-done.7 = s32[4,8]{1,0:T(4,128)S(1)} copy-done((s32[4,8]{1,0:T(4,128)S(1)}, s32[4,8]{1,0:T(4,128)}, u32[]{:S(2)}) %copy-start.7) | copy-done | bytes 152
  1.6 0.1 convert_element_type.31
  1.6 0.1 copy.28
  1.8 0.1 slice_bitcast_fusion.1
  1.9 0.1 copy.22
  1.9 0.1 copy.20
  2.1 21.4 %exchange.1 = (bf16[8,72,256]{2,1,0:T(8,128)(2,1)S(1)}, bf16[8,72,128]{2,1,0:T(8,128)(2,1)S(1)}, bf16[8,8,128]{2,1,0:T(8,128)(2,1)S(1)}) custom-call(bf16[72,256]{1,0:T(8,128)(2,1)S(1)} %fusion.11.pack_ref), custom_call_target="tpu_custom_call" | custom-call | tf_op jit(solution)/shard_map/exchange/pallas_call | solution.py:320
  23.5 0.1 convert_element_type.32
  23.6 0.1 reshape.48
  23.7 0.1 pad_convert_fusion
  23.7 0.1 constant_dynamic-slice_fusion.sh
  23.8 0.2 copy.25
  24.0 0.2 copy.24
  24.2 0.1 pad.28.clone
  24.3 0.1 pad_maximum_fusion.e_ref
  24.4 0.1 copy.27
  24.5 0.1 copy.26
  24.7 0.1 pad.25.clone
  24.8 0.1 pad_maximum_fusion.1.r_ref
  24.9 0.7 %copy-done.1 = bf16[8,8,3,3,3]{1,0,4,3,2:T(8,128)(2,1)S(1)} copy-done((bf16[8,8,3,3,3]{1,0,4,3,2:T(8,128)(2,1)S(1)}, bf16[8,8,3,3,3]{1,0,4,3,2:T(8,128)(2,1)}, u32[]{:S(2)}) %copy-start.1) | copy-done | bytes 3480
  25.6 7.9 %cost_volume.1 = bf16[8,8,4,256]{3,2,1,0:T(4,128)(2,1)} custom-call(s32[4,12]{1,0:T(4,128)S(1)} %constant_dynamic-slice_fusion.sh, bf16[8,72,256]{2,1,0:T(8,128)(2,1)S(1)} %get-tuple-element.8.g_ref, bf16[8,72,128]{2,1,0:T(8,128)(2,1)S(1)} %get-tuple-element.9.l_ref, bf16[8,4,16,128]{3,2,1,0:T(8,128)(2,1)S(1)} %pad_maximum_fusion.e_ref, ...), custom_call_target="tpu_custom_call" | custom-call | tf_op jit(solution)/shard_map/cost_volume/pallas_call | solution.py:188
  (25 shorter events, 0.2 us)
Async XLA Ops:
  0.8 1.0 %copy-start.6 = (bf16[32,4,256]{2,1,0:T(4,128)(2,1)S(1)}, bf16[32,4,256]{2,1,0:T(4,128)(2,1)}, u32[]{:S(2)}) copy-start(bf16[32,4,256]{2,1,0:T(4,128)(2,1)} %param.9) | copy-start | bytes 196612
  0.9 0.7 %copy-start.7 = (s32[4,8]{1,0:T(4,128)S(1)}, s32[4,8]{1,0:T(4,128)}, u32[]{:S(2)}) copy-start(s32[4,8]{1,0:T(4,128)} %param.11) | copy-start | bytes 388
  1.8 23.1 %copy-start = (bf16[1024,384]{1,0:T(8,128)(2,1)S(1)}, bf16[1024,384]{1,0:T(8,128)(2,1)}, u32[]{:S(2)}) copy-start(bf16[1024,384]{1,0:T(8,128)(2,1)} %constant.25.clone.place_ref) | copy-start | bytes 2359300
  24.8 0.8 %copy-start.1 = (bf16[8,8,3,3,3]{1,0,4,3,2:T(8,128)(2,1)S(1)}, bf16[8,8,3,3,3]{1,0,4,3,2:T(8,128)(2,1)}, u32[]{:S(2)}) copy-start(bf16[8,8,3,3,3]{1,0,4,3,2:T(8,128)(2,1)} %param.12) | copy-start | bytes 10372
  24.8 0.8 %copy-start.2 = (bf16[8,8,3,3,3]{1,0,4,3,2:T(8,128)(2,1)S(1)}, bf16[8,8,3,3,3]{1,0,4,3,2:T(8,128)(2,1)}, u32[]{:S(2)}) copy-start(bf16[8,8,3,3,3]{1,0,4,3,2:T(8,128)(2,1)} %param.14) | copy-start | bytes 10372
  24.9 0.8 %copy-start.3 = (f32[8]{0:T(128)S(1)}, f32[8]{0:T(128)}, u32[]{:S(2)}) copy-start(f32[8]{0:T(128)} %b1_ref.1) | copy-start | bytes 100
  24.9 0.7 %copy-start.4 = (f32[8]{0:T(128)S(1)}, f32[8]{0:T(128)}, u32[]{:S(2)}) copy-start(f32[8]{0:T(128)} %b2_ref.1) | copy-start | bytes 100
  24.9 0.7 %copy-start.5 = (f32[8]{0:T(128)S(1)}, f32[8]{0:T(128)}, u32[]{:S(2)}) copy-start(f32[8]{0:T(128)} %head_ref.1) | copy-start | bytes 100

commit v3 on v2

--- a/solution.py
+++ b/solution.py
@@ -42,14 +42,14 @@
         out_ref[do * 32 : do * 32 + 32, :] = pltpu.roll(base, 96 * do, 1).astype(BF16) if do else base.astype(BF16)
 
 
-def per_row(ref):
+def per_row(ref, k):
     low = lax.broadcasted_iota(jnp.int32, (8, 128), 0) < 4
-    return [jnp.where(low, ref[2 * q], ref[2 * q + 1]) for q in range(4)]
+    return [jnp.where(low, ref[k, 0, 2 * q], ref[k, 0, 2 * q + 1]) for q in range(4)]
 
 
 def compute(
-    plane_axis, tile_axis, sh, g_ref, l_ref, e_ref, r_ref, w1_ref, w2_ref, place_ref, b1_ref, b2_ref,
-    head_ref, o_ref, src2, rf, w1, w2, x2, f2, acc, tot,
+    plane_axis, tile_axis, small, sh, g_ref, l_ref, e_ref, r_ref, w1, w2, o_ref,
+    src2, rf, x2, f2, acc, tot,
 ):
     p = lax.axis_index(plane_axis)
     t = lax.axis_index(tile_axis)
@@ -59,11 +59,9 @@
     lane32 = lax.broadcasted_iota(jnp.int32, (32, 128), 1)
     sub = lax.broadcasted_iota(jnp.int32, (8, 128), 0)
     low = sub < 4
-    banded(w1_ref, place_ref, w1, 5)
-    banded(w2_ref, place_ref, w2, 4)
     for k in range(3):
         rf[k] = r_ref[:, k * 128 : k * 128 + 128].astype(F32) * 0.25
-    bias_one, bias_two, head = per_row(b1_ref), per_row(b2_ref), per_row(head_ref)
+    bias_one, bias_two, head = per_row(small, 0), per_row(small, 1), per_row(small, 2)
     edge_keep = jnp.where(
         jnp.logical_or(jnp.logical_and(lane == 0, t < last_t), jnp.logical_and(lane == 127, t > 0)), 1.0, 0.0
     )
@@ -86,10 +84,15 @@
         both = g_ref[:, own, :].reshape(128, 256)
         src[1] = both[:, :128]
         src[2] = both[:, 128:]
-        src[3] = e_ref[:, v].reshape(128, 128)
+        src[3] = e_ref[:, own, :].reshape(128, 128)
 
         def one_plane(d):
-            s = sh[v, d]
+            if d < 2:
+                s = sh[jnp.maximum(p - 1, 0) * 8 + 4 + v, 6 + d]
+            elif d > 9:
+                s = sh[jnp.minimum(p + 1, last_p) * 8 + 4 + v, d - 10]
+            else:
+                s = sh[p * 8 + 4 + v, d - 2]
             before = lane32 < s
             outer = jnp.logical_xor(before, lane32 < 64)
             parts = [[], [], []]
@@ -181,34 +184,52 @@
             o_ref[2 * q + 1, d] = val[4:8]
 
 
-def call_compute(plane_axis, tile_axis, sh, g, l, e, r, w1, w2, b1, b2, head):
+def call_compute(plane_axis, tile_axis, small, sh, g, l, e, r, w1, w2):
     smem = pl.BlockSpec(memory_space=pltpu.SMEM)
     vmem = pl.BlockSpec(memory_space=pltpu.VMEM)
-    place = jnp.asarray(placing(), BF16)
     return pl.pallas_call(
         functools.partial(compute, plane_axis, tile_axis),
         out_shape=jax.ShapeDtypeStruct((8, 8, 4, 256), BF16),
-        in_specs=[smem, vmem, vmem, vmem, vmem, vmem, vmem, vmem, smem, smem, smem],
+        in_specs=[smem, smem] + [vmem] * 6,
         out_specs=vmem,
         scratch_shapes=[
             pltpu.VMEM((4, 128, 128), BF16),
             pltpu.VMEM((3, 128, 128), F32),
-            pltpu.VMEM((160, 768), BF16),
-            pltpu.VMEM((128, 768), BF16),
             pltpu.VMEM((2, 1152, 384), BF16),
             pltpu.VMEM((2, 960, 256), BF16),
             pltpu.VMEM((8, 32, 256), F32),
             pltpu.VMEM((8, 8, 256), F32),
         ],
-        compiler_params=pltpu.CompilerParams(vmem_limit_bytes=40 << 20),
+        compiler_params=pltpu.CompilerParams(vmem_limit_bytes=60 * 1024 * 1024),
         name="cost_volume",
-    )(sh, g, l, e, r, w1, w2, place, b1, b2, head)
+    )(small, sh, g, l, e, r, w1, w2)
 
 
 MESH = pl.DeviceIdType.MESH
 
 
-def exchange(pack_ref, g_ref, l_ref, r_ref, send, recv, pass_send, pass_recv, own_sem):
+def marks(rows, pairs):
+    row = lax.broadcasted_iota(jnp.int32, (rows, 128), 0)
+    lane = lax.broadcasted_iota(jnp.int32, (rows, 128), 1)
+    hit = None
+    for r, l in pairs:
+        here = jnp.logical_and(row == r, lane == l)
+        hit = here if hit is None else jnp.logical_or(hit, here)
+    return jnp.where(hit, 1.0, 0.0).astype(BF16)
+
+
+def pick(mark, rows):
+    return lax.dot_general(mark, rows, (((1,), (1,)), ((), ())), preferred_element_type=F32)
+
+
+def unpick(rows, mark):
+    return lax.dot_general(rows, mark, (((0,), (0,)), ((), ())), preferred_element_type=F32)
+
+
+def exchange(
+    src_hbm, ref_hbm, sh_hbm, w1_hbm, w2_hbm, b1_hbm, b2_hbm, head_hbm, place_hbm, small_out, sh_out, g_ref, l_ref, e_ref, wide_ref, w1_out, w2_out,
+    src_raw, ref_raw, sh_ref, w_raw, place, pack_ref, r_ref, send, recv, pass_send, pass_recv, own_sem, load,
+):
     t, p = lax.axis_index("tile"), lax.axis_index("plane")
     last = lax.axis_size("tile") - 1
     chip, core = p // 2, p % 2
@@ -232,6 +253,33 @@
     for dz in range(4):
         greet(t, peers[dz])
 
+    loads = [
+        pltpu.make_async_copy(src_hbm, src_raw, load.at[0]),
+        pltpu.make_async_copy(ref_hbm, ref_raw, load.at[1]),
+        pltpu.make_async_copy(sh_hbm, sh_ref, load.at[2]),
+        pltpu.make_async_copy(w1_hbm, w_raw.at[0], load.at[3]),
+        pltpu.make_async_copy(w2_hbm, w_raw.at[1], load.at[4]),
+        pltpu.make_async_copy(place_hbm, place, load.at[5]),
+        pltpu.make_async_copy(b1_hbm, small_out.at[0], load.at[6]),
+        pltpu.make_async_copy(b2_hbm, small_out.at[1], load.at[7]),
+        pltpu.make_async_copy(head_hbm, small_out.at[2], load.at[8]),
+    ]
+    for one in loads:
+        one.start()
+    for one in loads[:3]:
+        one.wait()
+    own = src_raw[...].reshape(64, 256)
+    wide = ref_raw[...].reshape(128, 256)
+    whole = jnp.concatenate([own[:, :128], jnp.zeros((64, 128), BF16)], axis=0)
+    amounts = jnp.concatenate([sh_ref[...].astype(F32), jnp.zeros((4, 120), F32)], axis=1)
+    amounts = jnp.concatenate([jnp.zeros((4, 128), F32), amounts], axis=0)
+    head = pick(marks(8, ((0, 0), (1, 1))), whole) + pick(marks(8, ((2, 0), (3, 1))), wide[:, :128])
+    tail = pick(marks(8, ((0, 126), (1, 127))), whole) + pick(marks(8, ((2, 126), (3, 127))), wide[:, 128:])
+    pack_ref[0:64, :] = own
+    pack_ref[64:72, 0:128] = (head + amounts).astype(BF16)
+    pack_ref[64:72, 128:256] = tail.astype(BF16)
+    wide_ref[:, 0:256] = wide
+
     sides = jnp.where(t < last, 1, 0) + jnp.where(t > 0, 1, 0)
     pl.semaphore_wait(barrier, 4 + sides)
 
@@ -266,6 +314,11 @@
     for dz in (2, 1, 3, 0):
         spread(0, dz).start()
     mine.start()
+
+    for one in loads[3:]:
+        one.wait()
+    banded(w_raw.at[0], place, w1_out, 5)
+    banded(w_raw.at[1], place, w2_out, 4)
 
     @pl.when(t > 0)
     def _():
@@ -314,66 +367,70 @@
         finish(2)
         right.wait_send()
 
-
-def call_exchange(pack):
+    zero = jnp.zeros((8, 128), BF16)
+    sh_out[...] = g_ref[:, 64:72, 0:128].reshape(64, 128).astype(F32).astype(jnp.int32)
+
+    def edges(q):
+        after = jnp.where(t < last, r_ref[q], zero)
+        before = jnp.where(t > 0, l_ref[q, 64:72, :], zero)
+        return jnp.concatenate([after, before], axis=0)
+
+    mark = marks(16, ((0, 0), (1, 1), (8, 126), (9, 127)))
+    for q in range(8):
+        e_ref[q] = unpick(edges(q), mark)[:64].astype(BF16)
+    mark = marks(16, ((2, 0), (3, 1), (10, 126), (11, 127)))
+    wide_ref[:, 256:384] = unpick(edges(0), mark).astype(BF16)
+
+
+def call_exchange(src, ref, shifts, w1, w2, b1, b2, head):
     vmem = pl.BlockSpec(memory_space=pltpu.VMEM)
+    hbm = pl.BlockSpec(memory_space=pltpu.HBM)
+    place = jnp.asarray(placing(), BF16)
     return pl.pallas_call(
         exchange,
         out_shape=[
+            jax.ShapeDtypeStruct((3, 1, 8), F32),
+            jax.ShapeDtypeStruct((64, 128), jnp.int32),
             jax.ShapeDtypeStruct((8, 72, 256), BF16),
             jax.ShapeDtypeStruct((8, 72, 128), BF16),
-            jax.ShapeDtypeStruct((8, 8, 128), BF16),
+            jax.ShapeDtypeStruct((8, 64, 128), BF16),
+            jax.ShapeDtypeStruct((128, 384), BF16),
+            jax.ShapeDtypeStruct((160, 768), BF16),
+            jax.ShapeDtypeStruct((128, 768), BF16),
         ],
-        in_specs=[vmem],
-        out_specs=[vmem, vmem, vmem],
+        in_specs=[hbm] * 9,
+        out_specs=[vmem] * 8,
         scratch_shapes=[
+            pltpu.VMEM((4, 4, 4, 256), BF16),
+            pltpu.VMEM((32, 4, 256), BF16),
+            pltpu.VMEM((4, 8), jnp.int32),
+            pltpu.VMEM((2, 27, 8, 8), BF16),
+            pltpu.VMEM((1024, 384), BF16),
+            pltpu.VMEM((72, 256), BF16),
+            pltpu.VMEM((8, 8, 128), BF16),
             pltpu.SemaphoreType.DMA((3, 5)),
             pltpu.SemaphoreType.DMA((3, 5)),
             pltpu.SemaphoreType.DMA((3, 4)),
             pltpu.SemaphoreType.DMA((3, 4)),
             pltpu.SemaphoreType.DMA,
+            pltpu.SemaphoreType.DMA((9,)),
         ],
         compiler_params=pltpu.CompilerParams(
-            collective_id=0, has_side_effects=True, vmem_limit_bytes=8 << 20
+            collective_id=0, has_side_effects=True, vmem_limit_bytes=60 * 1024 * 1024
         ),
         name="exchange",
-    )(pack)
+    )(src, ref, shifts, w1, w2, b1, b2, head, place)
 
 
 def per_device(ref_feat, src_feat, shifts, conv_one, bias_one, conv_two, bias_two, view_head):
-    t, p = lax.axis_index("tile"), lax.axis_index("plane")
-    last_t = lax.axis_size("tile") - 1
-    ref_rows = ref_feat.reshape(128, 256)
-    src_rows = src_feat.reshape(64, 256)
-
-    def side(at, more):
-        lo = jnp.pad(src_rows[:, at : at + 2].T, ((0, 0), (0, 64)))
-        at = at if at == 0 else 254
-        hi = ref_rows[:, at : at + 2].T
-        return jnp.concatenate([lo, hi, more], axis=0)
-
-    whole = jnp.pad(shifts.reshape(1, 32).astype(BF16), ((0, 3), (0, 96)))
-    extra = jnp.concatenate([side(0, whole), side(126, jnp.zeros((4, 128), BF16))], axis=1)
-    pack = jnp.concatenate([src_rows, extra], axis=0)
-    g, l, r = call_exchange(pack)
-
-    def columns(rows):
-        return jnp.transpose(rows.reshape(8, 2, 4, 16), (0, 2, 3, 1))
-
-    el = columns(jnp.where(t > 0, l[:, 64:66, :64], 0))
-    er = columns(jnp.where(t < last_t, r[:, 0:2, :64], 0))
-    e = jnp.concatenate([er, jnp.zeros((8, 4, 16, 124), BF16), el], axis=-1)
-    rl = jnp.where(t > 0, l[0, 66:68, :], 0).T
-    rr = jnp.where(t < last_t, r[0, 2:4, :], 0).T
-    ref_wide = jnp.concatenate([ref_rows, rr, jnp.zeros((128, 124), BF16), rl], axis=1)
-    every = g[:, 68, :32].astype(jnp.int32).reshape(8, 4, 8)
-    every = jnp.pad(jnp.transpose(every, (1, 0, 2)).reshape(4, 64), ((0, 0), (2, 2)))
-    sh = lax.dynamic_slice_in_dim(every, p * 8, 12, 1)
-    kernel_of = lambda w: jnp.transpose(w, (2, 3, 4, 0, 1)).reshape(27, 8, 8)
-    return call_compute(
-        "plane", "tile", sh, g, l, e, ref_wide,
-        kernel_of(conv_one), kernel_of(conv_two), bias_one, bias_two, view_head,
+    def kernel_of(w):
+        return jnp.transpose(w, (2, 3, 4, 0, 1)).reshape(27, 8, 8)
+
+    shared = call_exchange(
+        src_feat, ref_feat, shifts, kernel_of(conv_one), kernel_of(conv_two),
+        bias_one.reshape(1, 8), bias_two.reshape(1, 8), view_head.reshape(1, 8),
     )
+    return call_compute("plane", "tile", *shared)
 
 
 def solution(mesh):

time: 33.8 us -> 31.3 us (0.926)
  local copies, waits for them, and re-layouts: 3.77 us -> 0 us
  Pallas kernels: 29.3 us -> 31.2 us
  other arithmetic: 0.34 us -> 0 us
    unnamed x18 -> x0, local copies, waits for them, and re-layouts: 1.5 us -> none
    pallas_call x1, Pallas kernels: 21.4 us -> 22.5 us  [call_exchange(): pl.pallas_call(exchange, out_shape=[jax.ShapeDtypeStruct((3, 1, 8), F32),...]
    reshape x3 -> x0, local copies, waits for them, and re-layouts: 0.89 us -> none  [the longest x1 0.77 us: per_device(): src_rows = src_feat.reshape(64, 256)]
    pallas_call x1, Pallas kernels: 7.9 us -> 8.65 us  [call_compute(): pl.pallas_call(functools.partial(compute, plane_axis, tile_axis), out_sha...]
    slice x6 -> x0, local copies, waits for them, and re-layouts: 0.39 us -> none  [the longest x2 0.14 us: per_device(): rr = jnp.where(t < last_t, r[0, 2:4, :], 0).T]
where the time goes in v3:
time: 31.3 us; the launch traced here: 31.2 us
  Pallas kernels  31.2 us (100%)
    pallas_call x1, Pallas kernels, call_exchange(): pl.pallas_call(exchange, out_shape=[jax.ShapeDtypeStruct((3, 1, 8), F32),...  22.5 us
    pallas_call x1, Pallas kernels, call_compute(): pl.pallas_call(functools.partial(compute, plane_axis, tile_axis), out_sha...  8.65 us

profile of v3, /device:TPU:129, one launch (start us, length us, event | category | flops | bytes accessed | tf_op | source)
XLA Modules:
  0.0 31.2 jit_solution(12904117796752845918)
XLA Ops:
  0.0 22.5 %exchange.1 = (f32[3,1,8]{2,1,0:T(1,128)}, s32[64,128]{1,0:T(8,128)}, bf16[8,72,256]{2,1,0:T(8,128)(2,1)}, bf16[8,72,128]{2,1,0:T(8,128)(2,1)}, bf16[8,64,128]{2...) custom-call(bf16[4,4,4,256]{3,2,1,0:T(4,128)(2,1)} %src_hbm.1, ...), custom_call_target="tpu_custom_call" | custom-call | tf_op jit(solution)/shard_map/exchange/pallas_call | solution.py:389
  22.5 8.6 %cost_volume.1 = bf16[8,8,4,256]{3,2,1,0:T(4,128)(2,1)} custom-call(f32[3,1,8]{2,1,0:T(1,128)} %get-tuple-element.13.small, s32[64,128]{1,0:T(8,128)} %get-tuple-element.14.sh, bf16[8,72,256]{2,1,0:T(8,128)(2,1)} %get-tuple-element.15.g_ref, bf16[8,72,128]{2,1,0:T(8,128)(2,1)} %get-tuple-element.16.l_ref, bf16[8,64,128]{2,1,0:T(8,128)(2,1)} %get-tuple-element.17.e_ref, ...), custom_call_target="tpu_custom_call" | custom-call | tf_op jit(solution)/shard_map/cost_volume/pallas_call | solution.py:190

commit v4 on v3

--- a/solution.py
+++ b/solution.py
@@ -7,6 +7,8 @@
 from jax.experimental.pallas import tpu as pltpu
 
 VIEWS = 4
+CONV_ONE = ((0, 3), (3, 3), (6, 2), (8, 2))
+CONV_TWO = ((0, 3), (3, 3), (6, 2))
 F32 = jnp.float32
 BF16 = jnp.bfloat16
 
@@ -37,7 +39,7 @@
         [jnp.where(which == ho, wide, 0.0) for ho in range(4)], axis=1
     ).astype(BF16)
     base = jnp.dot(wide, place_ref[...], preferred_element_type=F32)
-    base = jnp.concatenate([base, jnp.zeros((32, 384), F32)], axis=1)
+    base = jnp.concatenate([base, jnp.zeros((32, 128), F32)], axis=1)
     for do in range(steps):
         out_ref[do * 32 : do * 32 + 32, :] = pltpu.roll(base, 96 * do, 1).astype(BF16) if do else base.astype(BF16)
 
@@ -123,12 +125,14 @@
         for d in range(12):
             one_plane(d)
 
-        for j in range(2):
+        for first, count in CONV_ONE:
+            depth = (count + 2) * 96
             raw = jnp.dot(
-                w1[:, :672], x[j * 480 : j * 480 + 672, :], preferred_element_type=F32
+                w1[: count * 32, :depth], x[first * 96 : first * 96 + depth, :],
+                preferred_element_type=F32,
             )
-            for i in range(5):
-                d = j * 5 + i
+            for i in range(count):
+                d = first + i
                 tiles = []
                 for k in range(3):
                     cols = slice(k * 128, k * 128 + 128)
@@ -148,10 +152,14 @@
                     for k in range(2):
                         f[d * 96 + e * 32 : d * 96 + e * 32 + 32, k * 128 : k * 128 + 128] = moved[k]
 
-        for j in range(2):
-            raw = jnp.dot(w2[:, :576], f[j * 384 : j * 384 + 576, :], preferred_element_type=F32)
-            for i in range(4):
-                d = j * 4 + i
+        for first, count in CONV_TWO:
+            depth = (count + 2) * 96
+            raw = jnp.dot(
+                w2[: count * 32, :depth], f[first * 96 : first * 96 + depth, :],
+                preferred_element_type=F32,
+            )
+            for i in range(count):
+                d = first + i
                 for k in range(2):
                     cols = slice(k * 128, k * 128 + 128)
                     score = None
@@ -169,14 +177,12 @@
                         acc[d, rows, cols] = acc[d, rows, cols] + weight * match[rows]
 
     def two_views(i, carry):
-        for k in range(2):
-            one_view(i * 2 + k, x2.at[k], f2.at[k])
+        one_view(i, x2.at[0], f2.at[0])
         return carry
 
     acc[...] = jnp.zeros_like(acc)
     tot[...] = jnp.zeros_like(tot)
-    two_views(0, 0)
-    two_views(1, 0)
+    lax.fori_loop(0, VIEWS, two_views, 0)
     for d in range(8):
         for q in range(4):
             val = (acc[d, q * 8 : q * 8 + 8, :] / tot[d]).astype(BF16)
@@ -317,8 +323,8 @@
 
     for one in loads[3:]:
         one.wait()
-    banded(w_raw.at[0], place, w1_out, 5)
-    banded(w_raw.at[1], place, w2_out, 4)
+    banded(w_raw.at[0], place, w1_out, 3)
+    banded(w_raw.at[1], place, w2_out, 3)
 
     @pl.when(t > 0)
     def _():
@@ -395,8 +401,8 @@
             jax.ShapeDtypeStruct((8, 72, 128), BF16),
             jax.ShapeDtypeStruct((8, 64, 128), BF16),
             jax.ShapeDtypeStruct((128, 384), BF16),
-            jax.ShapeDtypeStruct((160, 768), BF16),
-            jax.ShapeDtypeStruct((128, 768), BF16),
+            jax.ShapeDtypeStruct((96, 512), BF16),
+            jax.ShapeDtypeStruct((96, 512), BF16),
         ],
         in_specs=[hbm] * 9,
         out_specs=[vmem] * 8,

time: 31.3 us -> 30.1 us (0.962)
  Pallas kernels: 31.2 us -> 30 us
    pallas_call x1, Pallas kernels: 8.65 us -> 7.46 us  [call_compute(): pl.pallas_call(functools.partial(compute, plane_axis, tile_axis), out_sha...]
where the time goes in v4:
time: 30.1 us; the launch traced here: 30 us
  Pallas kernels  30 us (100%)
    pallas_call x1, Pallas kernels, call_exchange(): pl.pallas_call(exchange, out_shape=[jax.ShapeDtypeStruct((3, 1, 8), F32),...  22.5 us
    pallas_call x1, Pallas kernels, call_compute(): pl.pallas_call(functools.partial(compute, plane_axis, tile_axis), out_sha...  7.46 us

profile of v4, /device:TPU:129, one launch (start us, length us, event | category | flops | bytes accessed | tf_op | source)
XLA Modules:
  0.0 30.0 jit_solution(4703541150454041239)
XLA Ops:
  0.0 22.5 %exchange.1 = (f32[3,1,8]{2,1,0:T(1,128)}, s32[64,128]{1,0:T(8,128)}, bf16[8,72,256]{2,1,0:T(8,128)(2,1)}, bf16[8,72,128]{2,1,0:T(8,128)(2,1)}, bf16[8,64,128]{2...) custom-call(bf16[4,4,4,256]{3,2,1,0:T(4,128)(2,1)} %src_hbm.1, ...), custom_call_target="tpu_custom_call" | custom-call | tf_op jit(solution)/shard_map/exchange/pallas_call | solution.py:395
  22.5 7.5 %cost_volume.1 = bf16[8,8,4,256]{3,2,1,0:T(4,128)(2,1)} custom-call(f32[3,1,8]{2,1,0:T(1,128)} %get-tuple-element.13.small, s32[64,128]{1,0:T(8,128)} %get-tuple-element.14.sh, bf16[8,72,256]{2,1,0:T(8,128)(2,1)} %get-tuple-element.15.g_ref, bf16[8,72,128]{2,1,0:T(8,128)(2,1)} %get-tuple-element.16.l_ref, bf16[8,64,128]{2,1,0:T(8,128)(2,1)} %get-tuple-element.17.e_ref, ...), custom_call_target="tpu_custom_call" | custom-call | tf_op jit(solution)/shard_map/cost_volume/pallas_call | solution.py:196

commit v5 on v4

--- a/solution.py
+++ b/solution.py
@@ -68,15 +68,13 @@
         jnp.logical_or(jnp.logical_and(lane == 0, t < last_t), jnp.logical_and(lane == 127, t > 0)), 1.0, 0.0
     )
 
-    def neighbours(tiles, lanes):
+    def neighbours(tiles, lanes, keep):
         n = len(tiles)
         tiles = [a.astype(BF16) for a in tiles]
-        right = [pltpu.roll(a, 1, 1) for a in tiles]
-        left = [pltpu.roll(a, 127, 1) for a in tiles]
         return (
-            [jnp.where(lanes == 0, right[(k - 1) % n], right[k]) for k in range(n)],
+            [pltpu.roll(jnp.where(lanes == 127, tiles[k - 1], tiles[k]), 1, 1) for k in range(keep)],
             tiles,
-            [jnp.where(lanes == 127, left[(k + 1) % n], left[k]) for k in range(n)],
+            [pltpu.roll(jnp.where(lanes == 0, tiles[(k + 1) % n], tiles[k]), 127, 1) for k in range(keep)],
         )
 
     def one_view(v, xs, f):
@@ -95,17 +93,20 @@
                 s = sh[jnp.minimum(p + 1, last_p) * 8 + 4 + v, d - 10]
             else:
                 s = sh[p * 8 + 4 + v, d - 2]
-            before = lane32 < s
-            outer = jnp.logical_xor(before, lane32 < 64)
+            lands = (lane32 + s) & 127
+            before = lands < s
+            first_half = lands < 64
+            outer = jnp.logical_xor(before, first_half)
             parts = [[], [], []]
             for q in range(4):
                 rows = slice(32 * q, 32 * q + 32)
-                r = [pltpu.roll(src[k, rows, :], s, 1) for k in range(4)]
+                r = [src[k, rows, :] for k in range(4)]
                 tiles = (
                     jnp.where(before, r[0], r[1]),
                     jnp.where(before, r[1], r[2]),
-                    jnp.where(outer, r[3], jnp.where(lane32 < 64, r[2], r[0])),
+                    jnp.where(outer, r[3], jnp.where(first_half, r[2], r[0])),
                 )
+                tiles = [pltpu.roll(a, s, 1) for a in tiles]
                 for k in range(3):
                     prod = tiles[k].astype(F32) * rf[k, rows, :]
                     v0 = prod[0:8] + prod[8:16]
@@ -118,7 +119,7 @@
             if d > 9:
                 tiles = [jnp.where(p < last_p, a, 0.0) for a in tiles]
             base = d * 96
-            for e, moved in enumerate(neighbours(tiles, lane32)):
+            for e, moved in enumerate(neighbours(tiles, lane32, 3)):
                 for k in range(3):
                     x[base + e * 32 : base + e * 32 + 32, k * 128 : k * 128 + 128] = moved[k]
 
@@ -148,7 +149,7 @@
                             val = jnp.where(p < last_p, val, 0.0)
                         rows.append(val)
                     tiles.append(jnp.concatenate(rows, axis=0))
-                for e, moved in enumerate(neighbours(tiles, lane32)):
+                for e, moved in enumerate(neighbours(tiles, lane32, 2)):
                     for k in range(2):
                         f[d * 96 + e * 32 : d * 96 + e * 32 + 32, k * 128 : k * 128 + 128] = moved[k]
 

time: 30.1 us -> 29.6 us (0.983)
  Pallas kernels: 30 us -> 29.4 us
    pallas_call x1, Pallas kernels: 7.46 us -> 6.93 us  [call_compute(): pl.pallas_call(functools.partial(compute, plane_axis, tile_axis), out_sha...]
where the time goes in v5:
time: 29.6 us; the launch traced here: 29.4 us
  Pallas kernels  29.4 us (99%)
    pallas_call x1, Pallas kernels, call_exchange(): pl.pallas_call(exchange, out_shape=[jax.ShapeDtypeStruct((3, 1, 8), F32),...  22.5 us
    pallas_call x1, Pallas kernels, call_compute(): pl.pallas_call(functools.partial(compute, plane_axis, tile_axis), out_sha...  6.93 us

profile of v5, /device:TPU:129, one launch (start us, length us, event | category | flops | bytes accessed | tf_op | source)
XLA Modules:
  0.0 29.4 jit_solution(13544047830309691662)
XLA Ops:
  0.0 22.5 %exchange.1 = (f32[3,1,8]{2,1,0:T(1,128)}, s32[64,128]{1,0:T(8,128)}, bf16[8,72,256]{2,1,0:T(8,128)(2,1)}, bf16[8,72,128]{2,1,0:T(8,128)(2,1)}, bf16[8,64,128]{2...) custom-call(bf16[4,4,4,256]{3,2,1,0:T(4,128)(2,1)} %src_hbm.1, ...), custom_call_target="tpu_custom_call" | custom-call | tf_op jit(solution)/shard_map/exchange/pallas_call | solution.py:396
  22.5 6.9 %cost_volume.1 = bf16[8,8,4,256]{3,2,1,0:T(4,128)(2,1)} custom-call(f32[3,1,8]{2,1,0:T(1,128)} %get-tuple-element.13.small, s32[64,128]{1,0:T(8,128)} %get-tuple-element.14.sh, bf16[8,72,256]{2,1,0:T(8,128)(2,1)} %get-tuple-element.15.g_ref, bf16[8,72,128]{2,1,0:T(8,128)(2,1)} %get-tuple-element.16.l_ref, bf16[8,64,128]{2,1,0:T(8,128)(2,1)} %get-tuple-element.17.e_ref, ...), custom_call_target="tpu_custom_call" | custom-call | tf_op jit(solution)/shard_map/cost_volume/pallas_call | solution.py:197

commit v6 on v5

--- a/solution.py
+++ b/solution.py
@@ -8,7 +8,7 @@
 
 VIEWS = 4
 CONV_ONE = ((0, 3), (3, 3), (6, 2), (8, 2))
-CONV_TWO = ((0, 3), (3, 3), (6, 2))
+CONV_TWO = ((0, 2), (2, 2), (4, 2), (6, 2))
 F32 = jnp.float32
 BF16 = jnp.bfloat16
 
@@ -327,18 +327,6 @@
     banded(w_raw.at[0], place, w1_out, 3)
     banded(w_raw.at[1], place, w2_out, 3)
 
-    @pl.when(t > 0)
-    def _():
-        right.wait_recv()
-        for dz in (2, 1, 3, 0):
-            spread(1, dz).start()
-
-    @pl.when(t < last)
-    def _():
-        left.wait_recv()
-        for dz in (2, 1, 3, 0):
-            spread(2, dz).start()
-
     def relay(kind):
         for dz in (1, 3, 2):
             spread(kind, dz).wait_recv()
@@ -351,14 +339,41 @@
         for dz in (1, 3, 2):
             passing(kind, dz).wait()
 
+    near_left, near_right = lax.rem(t, 16) != 0, lax.rem(t + 1, 16) != 0
+
+    def onward(kind, arrival):
+        arrival.wait_recv()
+        for dz in (2, 1, 3, 0):
+            spread(kind, dz).start()
+
+    from_left, from_right = t > 0, t < last
+
+    @pl.when(jnp.logical_and(from_left, near_left))
+    def _():
+        onward(1, right)
+
+    @pl.when(jnp.logical_and(from_right, near_right))
+    def _():
+        onward(2, left)
+
     relay(0)
 
-    @pl.when(t > 0)
+    @pl.when(jnp.logical_and(from_left, near_left))
     def _():
         relay(1)
 
-    @pl.when(t < last)
-    def _():
+    @pl.when(jnp.logical_and(from_right, near_right))
+    def _():
+        relay(2)
+
+    @pl.when(jnp.logical_and(from_left, jnp.logical_not(near_left)))
+    def _():
+        onward(1, right)
+        relay(1)
+
+    @pl.when(jnp.logical_and(from_right, jnp.logical_not(near_right)))
+    def _():
+        onward(2, left)
         relay(2)
 
     mine.wait()

time: 29.6 us -> 29.5 us (level)
  no operation moved by 1% of the time
where the time goes in v6:
time: 29.5 us; the launch traced here: 29.4 us
  Pallas kernels  29.4 us (100%)
    pallas_call x1, Pallas kernels, call_exchange(): pl.pallas_call(exchange, out_shape=[jax.ShapeDtypeStruct((3, 1, 8), F32),...  22.4 us
    pallas_call x1, Pallas kernels, call_compute(): pl.pallas_call(functools.partial(compute, plane_axis, tile_axis), out_sha...  6.98 us

profile of v6, /device:TPU:129, one launch (start us, length us, event | category | flops | bytes accessed | tf_op | source)
XLA Modules:
  0.0 29.4 jit_solution(14920481156297474875)
XLA Ops:
  0.0 22.4 %exchange.1 = (f32[3,1,8]{2,1,0:T(1,128)}, s32[64,128]{1,0:T(8,128)}, bf16[8,72,256]{2,1,0:T(8,128)(2,1)}, bf16[8,72,128]{2,1,0:T(8,128)(2,1)}, bf16[8,64,128]{2...) custom-call(bf16[4,4,4,256]{3,2,1,0:T(4,128)(2,1)} %src_hbm.1, ...), custom_call_target="tpu_custom_call" | custom-call | tf_op jit(solution)/shard_map/exchange/pallas_call | solution.py:411
  22.4 7.0 %cost_volume.1 = bf16[8,8,4,256]{3,2,1,0:T(4,128)(2,1)} custom-call(f32[3,1,8]{2,1,0:T(1,128)} %get-tuple-element.13.small, s32[64,128]{1,0:T(8,128)} %get-tuple-element.14.sh, bf16[8,72,256]{2,1,0:T(8,128)(2,1)} %get-tuple-element.15.g_ref, bf16[8,72,128]{2,1,0:T(8,128)(2,1)} %get-tuple-element.16.l_ref, bf16[8,64,128]{2,1,0:T(8,128)(2,1)} %get-tuple-element.17.e_ref, ...), custom_call_target="tpu_custom_call" | custom-call | tf_op jit(solution)/shard_map/cost_volume/pallas_call | solution.py:197
